TPU v7x, 128 devices: a whole 4x4x4 slice. The times are simulated.
128 devices in a mesh: src: 8 (over y, core), tgt: 16 (over z, x).
Axes of the slice: x: 4, y: 4, z: 4, core: 2. Of those that a mesh axis runs over, the one named last changes fastest.
Arguments:
- src_vel: bfloat16 [2, 48, 524288], P(None, None, ('src', 'tgt')), may hold values from -6 to 6
- angle: float32 [524288], P(('src', 'tgt')), may hold values from -3.140625 to 3.140625
- src_block: int32 [8, 16, 16, 8], P('src', 'tgt'), may hold values from 0 to 31
- tgt_block: int32 [8, 16, 16, 8], P('src', 'tgt'), may hold values from 0 to 31
- send_count: int32 [8, 16, 16], P('src', 'tgt'), may hold values from 0 to 8, as said below
- intersection: bfloat16 [8, 16, 16, 8, 128, 128], P('src', 'tgt'), may hold values from -0.375 to 0.375
- eofs: bfloat16 [512, 2, 524288], P(None, None, ('src', 'tgt')), may hold values from -0.0234375 to 0.0234375
Outputs:
- remapped: bfloat16 [2, 48, 524288], P(None, None, ('src', 'tgt'))
- pcs: float32 [48, 512], P(None, 'tgt')
Inputs may be any that keep to these rules, and one draw needn't show every extreme that they name: `src_block`: indices of the sending device's own source blocks. `tgt_block`: indices of the receiving device's target blocks. `send_count`: in every tile row, one receiver column gets 8 live slots from every sender of the row.
All inputs are finite; a program needn't handle non-finite values.
Results may differ from a plain program's by a relative error of at most 0.0058.
Values may be sent and summed in bfloat16 or wider, within the bound.
No kernel may reach another device: no remote copies, remote signals or barrier semaphores. Data moves between devices by JAX's collectives and lax.ppermute only.
A program may use at most 64 MiB of HBM per device.

v0:
```python
import jax
import jax.numpy as jnp
from jax import lax
from jax.sharding import PartitionSpec as P

BLK = 128


def partner(x, axis, distance):
    return lax.ppermute(x, axis, [(i, i ^ 1 << distance) for i in range(lax.axis_size(axis))])


def split_up(x, dim, size):
    lengths = x.shape
    blocks = x.reshape(*lengths[:dim], size, lengths[dim] // size, *lengths[dim + 1 :])
    return jnp.moveaxis(blocks, dim, 0)


def sum_at_owner(x, axis, dim):
    size = lax.axis_size(axis)
    blocks = lax.all_to_all(split_up(x, dim, size), axis, 0, 0, tiled=True)
    return jnp.sum(blocks, axis=0)


def copy_for_each(x, axis):
    size = lax.axis_size(axis)
    return lax.all_to_all(jnp.broadcast_to(x[None], (size, *x.shape)), axis, 0, 0, tiled=True)


def taken_together(x, axis):
    return copy_for_each(x, axis).sum(axis=0)


def accumulate(received, recv_ids, tgt_blocks):
    slot_total = recv_ids.shape[0] * recv_ids.shape[1]
    row_count = received.shape[3]
    onehot = (
        recv_ids.reshape(1, slot_total)
        == lax.broadcasted_iota(jnp.int32, (tgt_blocks, slot_total), 0)
    ).astype(jnp.bfloat16)
    flat_recv = received.reshape(slot_total, 2, row_count, BLK)
    return jnp.einsum("bp,pctj->ctbj", onehot, flat_recv, preferred_element_type=jnp.float32)


def per_device(src_vel, angle, src_block, tgt_block, send_count, intersection, eofs):
    components, tl_rows, cell_count = src_vel.shape
    src_blocks = cell_count // BLK
    tgt_count = lax.axis_size("tgt")
    mirror = src_vel[:, :, cell_count - BLK :]
    for bit_index in range(tgt_count.bit_length() - 1):
        mirror = partner(mirror, "tgt", bit_index)
    velocity = src_vel.astype(jnp.float32)
    own_fold = velocity[:, :, cell_count - BLK :]
    folded = 0.5 * (own_fold - mirror[:, :, ::-1].astype(jnp.float32))
    at_top = lax.axis_index("src") == lax.axis_size("src") - 1
    velocity = velocity.at[:, :, cell_count - BLK :].set(jnp.where(at_top, folded, own_fold))
    cosine = jnp.cos(angle)
    sine_part = jnp.sin(angle)
    eastward = cosine * velocity[0] - sine_part * velocity[1]
    northward = sine_part * velocity[0] + cosine * velocity[1]
    rotated = (
        jnp.stack([eastward, northward])
        .astype(jnp.bfloat16)
        .reshape(components, tl_rows, src_blocks, BLK)
    )
    slot_cap = src_block.shape[3]
    slot_total = tgt_count * slot_cap
    blocks = jnp.take(rotated, src_block.reshape(slot_total), axis=2)
    weights = intersection.reshape(slot_total, BLK, BLK)
    contribs = jnp.einsum("ctpi,pij->pctj", blocks, weights, preferred_element_type=jnp.float32)
    contribs = contribs.astype(jnp.bfloat16).reshape(tgt_count, slot_cap, components, tl_rows, BLK)
    tgt_blocks = eofs.shape[2] // BLK
    live_slot = lax.broadcasted_iota(jnp.int32, (tgt_count, slot_cap), 1) < send_count.reshape(
        tgt_count, 1
    )
    slot_ids = jnp.where(live_slot, tgt_block.reshape(tgt_count, slot_cap), tgt_blocks)
    received, recv_ids = (
        lax.all_to_all(contribs, "tgt", split_axis=0, concat_axis=0, tiled=True),
        lax.all_to_all(slot_ids, "tgt", split_axis=0, concat_axis=0, tiled=True),
    )
    summed = accumulate(received, recv_ids, tgt_blocks)
    remapped = summed.reshape(components, tl_rows, tgt_blocks * BLK).astype(jnp.bfloat16)
    partial_value = jnp.einsum("ctn,kcn->tk", remapped, eofs, preferred_element_type=jnp.float32)
    column_part = sum_at_owner(partial_value, "tgt", 1)
    pcs = taken_together(column_part, "src")
    return (remapped, pcs)


def solution(mesh):
    return jax.shard_map(
        per_device,
        mesh=mesh,
        in_specs=(
            P(None, None, ("src", "tgt")),
            P(("src", "tgt")),
            P("src", "tgt", None, None),
            P("src", "tgt", None, None),
            P("src", "tgt", None),
            P("src", "tgt", None, None, None, None),
            P(None, None, ("src", "tgt")),
        ),
        out_specs=(P(None, None, ("src", "tgt")), P(None, "tgt")),
        check_vma=False,
    )
```

profile of v0, /device:TPU:1, one launch (start us, length us, event | category | flops | bytes accessed | tf_op | source)
XLA Modules:
  0.0 119.8 jit_solution(16252488181414294882)
XLA Ops:
  0.6 0.7 slice.37
  1.4 2.0 %collective-permute-start = (bf16[2,48,128]{2,1,0:T(8,128)(2,1)S(1)}, bf16[2,48,128]{2,1,0:T(8,128)(2,1)S(1)}, u32[]{:S(2)}, u32[]{:S(2)}) collective-permute-start(bf16[2,48,128]{2,1,0:T(8,128)(2,1)S(1)} %slice.37), channel_id=1, source_target_pairs={{0,1},{1,0},{2,3},{3,2},{4,5},{5,4},{6,7},{7,6},{8,9},{9,8},{10,11... | collective-permute-start | bytes 73736 | tf_op jit(solution)/shard_map/ppermute | solution.py:10
  3.4 0.7 bitcast_select_fusion
  4.1 0.7 copy.31
  4.8 7.3 %all-to-all-start.1 = ((s32[16,1,8]{2,1,0:T(1,128)}), s32[16,1,8]{2,1,0:T(1,128)S(1)}, u32[]{:S(2)}, u32[]{:S(2)}) async-start(s32[16,1,8]{2,1,0:T(1,128)} %copy.31), calls=%async_computation.1 | async-start | bytes 16384 | tf_op jit(solution)/shard_map/all_to_all | solution.py:79
  12.1 0.8 fusion.29
  12.9 0.8 copy.26
  13.7 2.9 %collective-permute-start.1 = (bf16[2,48,128]{2,1,0:T(8,128)(2,1)S(1)}, bf16[2,48,128]{2,1,0:T(8,128)(2,1)S(1)}, u32[]{:S(2)}, u32[]{:S(2)}) collective-permute-start(bf16[2,48,128]{2,1,0:T(8,128)(2,1)S(1)} %collective-permute-done), channel_id=1, source_target_pairs={{0,2},{1,3},{2,0},{3,1},{4,6},{5,7},{6,4},{7,5},{8,10},{9,11},{10,... | collective-permute-start | bytes 73736 | tf_op jit(solution)/shard_map/ppermute | solution.py:10
  16.8 1.3 %collective-permute-done.1 = bf16[2,48,128]{2,1,0:T(8,128)(2,1)S(1)} collective-permute-done((bf16[2,48,128]{2,1,0:T(8,128)(2,1)S(1)}, bf16[2,48,128]{2,1,0:T(8,128)(2,1)S(1)}, u32[]{:S(2)}, u32[]{:S(2)}) %collective-permute-start.1) | collective-permute-done | bytes 24608 | tf_op jit(solution)/shard_map/ppermute | solution.py:10
  18.0 1.3 %collective-permute-start.2 = (bf16[2,48,128]{2,1,0:T(8,128)(2,1)S(1)}, bf16[2,48,128]{2,1,0:T(8,128)(2,1)S(1)}, u32[]{:S(2)}, u32[]{:S(2)}) collective-permute-start(bf16[2,48,128]{2,1,0:T(8,128)(2,1)S(1)} %collective-permute-done.1), channel_id=1, source_target_pairs={{0,4},{1,5},{2,6},{3,7},{4,0},{5,1},{6,2},{7,3},{8,12},{9,13},{10,... | collective-permute-start | bytes 73736 | tf_op jit(solution)/shard_map/ppermute | solution.py:10
  19.4 1.3 %collective-permute-done.2 = bf16[2,48,128]{2,1,0:T(8,128)(2,1)S(1)} collective-permute-done((bf16[2,48,128]{2,1,0:T(8,128)(2,1)S(1)}, bf16[2,48,128]{2,1,0:T(8,128)(2,1)S(1)}, u32[]{:S(2)}, u32[]{:S(2)}) %collective-permute-start.2) | collective-permute-done | bytes 24608 | tf_op jit(solution)/shard_map/ppermute | solution.py:10
  20.7 3.1 %collective-permute-start.3 = (bf16[2,48,128]{2,1,0:T(8,128)(2,1)S(1)}, bf16[2,48,128]{2,1,0:T(8,128)(2,1)S(1)}, u32[]{:S(2)}, u32[]{:S(2)}) collective-permute-start(bf16[2,48,128]{2,1,0:T(8,128)(2,1)S(1)} %collective-permute-done.2), channel_id=1, source_target_pairs={{0,8},{1,9},{2,10},{3,11},{4,12},{5,13},{6,14},{7,15},{8,0},{9,1},... | collective-permute-start | bytes 73736 | tf_op jit(solution)/shard_map/ppermute | solution.py:10
  23.9 1.3 %convert_element_type.23 = f32[2,48,4096]{2,1,0:T(8,128)S(1)} convert(bf16[2,48,4096]{2,1,0:T(8,128)(2,1)} %param.9) | non-fusion elementwise | flops 393216 | bytes 2359296 | tf_op jit(solution)/shard_map/convert_element_type | solution.py:52
  25.7 2.6 %gather_fusion = bf16[128,2,48,128]{3,2,1,0:T(8,128)(2,1)} fusion(bf16[2,48,32,128]{3,1,2,0:T(8,128)(2,1)S(1)} %pad_maximum_fusion, s32[1024]{0:T(1024)S(1)} %pad_clamp_fusion), kind=kCustom, calls=%fused_computation | custom fusion | bytes 6291968 | tf_op jit(solution)/shard_map/jit(_take)/gather | solution.py:68
  28.3 6.1 %fusion.9 = bf16[128,2,48,128]{3,2,1,0:T(8,128)(2,1)} fusion(bf16[128,128,128,1]{2,1,3,0:T(8,128)(2,1)} %bitcast.66, bf16[128,2,48,128]{3,2,1,0:T(8,128)(2,1)} %gather_fusion, pred[128]{0:T(512)(128)(4,1)S(1)} %compare_and_fusion), kind=kOutput, calls=%fused_computation.10 | convolution fusion | flops 405798912 | bytes 10485888 | tf_op jit(solution)/shard_map/ctpi,pij->pctj/dot_general | solution.py:70
  34.5 6.4 %all-to-all-start = ((bf16[16,8,2,48,128]{4,3,2,1,0:T(8,128)(2,1)}), bf16[16,8,2,48,128]{4,3,2,1,0:T(8,128)(2,1)S(1)}, u32[]{:S(2)}, u32[]{:S(2)}) async-start(bf16[16,8,2,48,128]{4,3,2,1,0:T(8,128)(2,1)} %bitcast.65), calls=%async_computation | async-start | bytes 6291456 | tf_op jit(solution)/shard_map/all_to_all | solution.py:78
  40.9 0.5 broadcast.104
  41.4 0.7 reduce.5
  42.2 34.4 %all-to-all-done = bf16[16,8,2,48,128]{4,3,2,1,0:T(8,128)(2,1)S(1)} async-done(((bf16[16,8,2,48,128]{4,3,2,1,0:T(8,128)(2,1)}), bf16[16,8,2,48,128]{4,3,2,1,0:T(8,128)(2,1)S(1)}, u32[]{:S(2)}, u32[]{:S(2)}) %all-to-all-start) | async-done | bytes 3145760 | tf_op jit(solution)/shard_map/all_to_all | solution.py:78
  76.6 2.0 %fusion.16 = bf16[2,48,32,128]{3,2,1,0:T(8,128)(2,1)} fusion(bf16[16,8,2,48,128]{4,3,2,1,0:T(8,128)(2,1)S(1)} %all-to-all-done, s32[128]{0:T(128)S(1)} %eq.14), kind=kOutput, calls=%fused_computation.13 | convolution fusion | flops 101060608 | bytes 3932672 | tf_op jit(solution)/shard_map/bp,pctj->ctbj/dot_general | solution.py:42
  78.6 1.4 %reshape.189 = bf16[2,48,4096,1]{2,1,0,3:T(8,128)(2,1)S(1)} reshape(bf16[2,48,32,128]{3,2,1,0:T(8,128)(2,1)} %fusion.16) | data formatting | bytes 1572864 | tf_op jit(solution)/shard_map/convert_element_type | solution.py:82
  80.1 8.0 %fusion.30 = f32[16,32,48]{2,1,0:T(8,128)S(1)} fusion(bf16[2,48,4096,1]{2,1,0,3:T(8,128)(2,1)S(1)} %reshape.189, bf16[16,32,2,4096]{3,2,1,0:T(2,128)(2,1)} %bitcast.68), kind=kOutput, calls=%fused_computation.35 | convolution fusion | flops 402653184 | bytes 9273344 | tf_op jit(solution)/shard_map/ctn,kcn->tk/dot_general | solution.py:83
  88.1 0.3 reshape.201
  88.3 16.0 %all_to_all.21 = f32[16,1,1536]{2,1,0:T(1,128)S(1)} all-to-all(f32[16,1,1536]{2,1,0:T(1,128)S(1)} %reshape.201), channel_id=1, replica_groups=mesh['src'=8,'tgt'=16] {'tgt'}, dimensions={0} | all-to-all | bytes 196608 | tf_op jit(solution)/shard_map/all_to_all | solution.py:21
  104.4 0.5 broadcast.105
  104.9 0.9 reduce.6
  105.9 0.8 reshape.203
  106.7 6.8 %all-to-all-start.3 = ((f32[8,1,1536]{2,1,0:T(1,128)}), f32[8,1,1536]{2,1,0:T(1,128)S(1)}, u32[]{:S(2)}, u32[]{:S(2)}) async-start(f32[8,1,1536]{2,1,0:T(1,128)} %reshape.203), calls=%async_computation.3 | async-start | bytes 98304 | tf_op jit(solution)/shard_map/all_to_all | solution.py:27
  113.5 1.2 %convert_element_type.28 = bf16[2,48,4096]{2,1,0:T(8,128)(2,1)} reshape(bf16[2,48,32,128]{3,2,1,0:T(8,128)(2,1)S(1)} %copy-done) | data formatting | bytes 1572864 | tf_op jit(solution)/shard_map/convert_element_type | solution.py:82
  114.7 3.6 %all-to-all-done.3 = f32[8,1,1536]{2,1,0:T(1,128)S(1)} async-done(((f32[8,1,1536]{2,1,0:T(1,128)}), f32[8,1,1536]{2,1,0:T(1,128)S(1)}, u32[]{:S(2)}, u32[]{:S(2)}) %all-to-all-start.3) | async-done | bytes 49184 | tf_op jit(solution)/shard_map/all_to_all | solution.py:27
  118.3 0.8 reduce.7
  119.2 0.6 bitcast_reduce_fusion.1
  (20 shorter events, 1.1 us)
Async XLA Ops:
  1.4 12.4 %collective-permute-start = (bf16[2,48,128]{2,1,0:T(8,128)(2,1)S(1)}, bf16[2,48,128]{2,1,0:T(8,128)(2,1)S(1)}, u32[]{:S(2)}, u32[]{:S(2)}) collective-permute-start(bf16[2,48,128]{2,1,0:T(8,128)(2,1)S(1)} %slice.37), channel_id=1, source_target_pairs={{0,1},{1,0},{2,3},{3,2},{4,5},{5,4},{6,7},{7,6},{8,9},{9,8},{10,11... | collective-permute-start | bytes 73736 | tf_op jit(solution)/shard_map/ppermute | solution.py:10
  4.8 29.7 %all-to-all-start.1 = ((s32[16,1,8]{2,1,0:T(1,128)}), s32[16,1,8]{2,1,0:T(1,128)S(1)}, u32[]{:S(2)}, u32[]{:S(2)}) async-start(s32[16,1,8]{2,1,0:T(1,128)} %copy.31), calls=%async_computation.1 | async-start | bytes 16384 | tf_op jit(solution)/shard_map/all_to_all | solution.py:79
  13.7 4.3 %collective-permute-start.1 = (bf16[2,48,128]{2,1,0:T(8,128)(2,1)S(1)}, bf16[2,48,128]{2,1,0:T(8,128)(2,1)S(1)}, u32[]{:S(2)}, u32[]{:S(2)}) collective-permute-start(bf16[2,48,128]{2,1,0:T(8,128)(2,1)S(1)} %collective-permute-done), channel_id=1, source_target_pairs={{0,2},{1,3},{2,0},{3,1},{4,6},{5,7},{6,4},{7,5},{8,10},{9,11},{10,... | collective-permute-start | bytes 73736 | tf_op jit(solution)/shard_map/ppermute | solution.py:10
  18.0 2.7 %collective-permute-start.2 = (bf16[2,48,128]{2,1,0:T(8,128)(2,1)S(1)}, bf16[2,48,128]{2,1,0:T(8,128)(2,1)S(1)}, u32[]{:S(2)}, u32[]{:S(2)}) collective-permute-start(bf16[2,48,128]{2,1,0:T(8,128)(2,1)S(1)} %collective-permute-done.1), channel_id=1, source_target_pairs={{0,4},{1,5},{2,6},{3,7},{4,0},{5,1},{6,2},{7,3},{8,12},{9,13},{10,... | collective-permute-start | bytes 73736 | tf_op jit(solution)/shard_map/ppermute | solution.py:10
  20.7 4.4 %collective-permute-start.3 = (bf16[2,48,128]{2,1,0:T(8,128)(2,1)S(1)}, bf16[2,48,128]{2,1,0:T(8,128)(2,1)S(1)}, u32[]{:S(2)}, u32[]{:S(2)}) collective-permute-start(bf16[2,48,128]{2,1,0:T(8,128)(2,1)S(1)} %collective-permute-done.2), channel_id=1, source_target_pairs={{0,8},{1,9},{2,10},{3,11},{4,12},{5,13},{6,14},{7,15},{8,0},{9,1},... | collective-permute-start | bytes 73736 | tf_op jit(solution)/shard_map/ppermute | solution.py:10
  34.5 42.1 %all-to-all-start = ((bf16[16,8,2,48,128]{4,3,2,1,0:T(8,128)(2,1)}), bf16[16,8,2,48,128]{4,3,2,1,0:T(8,128)(2,1)S(1)}, u32[]{:S(2)}, u32[]{:S(2)}) async-start(bf16[16,8,2,48,128]{4,3,2,1,0:T(8,128)(2,1)} %bitcast.65), calls=%async_computation | async-start | bytes 6291456 | tf_op jit(solution)/shard_map/all_to_all | solution.py:78
  80.0 33.4 %copy-start = (bf16[2,48,32,128]{3,2,1,0:T(8,128)(2,1)S(1)}, bf16[2,48,32,128]{3,2,1,0:T(8,128)(2,1)}, u32[]{:S(2)}) copy-start(bf16[2,48,32,128]{3,2,1,0:T(8,128)(2,1)} %fusion.16) | copy-start | bytes 2359300
  106.7 11.6 %all-to-all-start.3 = ((f32[8,1,1536]{2,1,0:T(1,128)}), f32[8,1,1536]{2,1,0:T(1,128)S(1)}, u32[]{:S(2)}, u32[]{:S(2)}) async-start(f32[8,1,1536]{2,1,0:T(1,128)} %reshape.203), calls=%async_computation.3 | async-start | bytes 98304 | tf_op jit(solution)/shard_map/all_to_all | solution.py:27
where the time goes:
time: 120 us
  waiting for transfers between devices  40.6 us (34%)
  starting transfers between devices  29.9 us (25%)
  matrix products  16.2 us (14%)
  blocking collectives  16 us (13%)
  local copies, waits for them, and re-layouts  11 us (9%)
  other arithmetic  5.23 us (4%)
    all_to_all x1, waiting for transfers between devices, per_device(): lax.all_to_all(contribs, 'tgt', split_axis=0, concat_axis=0, tiled=True)  34.4 us
    all_to_all x1, blocking collectives, sum_at_owner(): blocks = lax.all_to_all(split_up(x, dim, size), axis, 0, 0, tiled=True)  16 us
    ppermute x4, starting transfers between devices, partner(): lax.ppermute(x, axis, [(i, i ^ 1 << distance) for i in range(lax.axis_siz...  9.45 us
    dot_general x1, matrix products, per_device(): jnp.einsum('ctn,kcn->tk', remapped, eofs, preferred_element_type=jnp.floa...  8 us
    all_to_all x1, starting transfers between devices, per_device(): lax.all_to_all(slot_ids, 'tgt', split_axis=0, concat_axis=0, tiled=True)  7.3 us
    all_to_all x1, starting transfers between devices, copy_for_each(): lax.all_to_all(jnp.broadcast_to(x[None], (size, *x.shape)), axis, 0, 0, t...  6.78 us
    all_to_all x1, starting transfers between devices, per_device(): lax.all_to_all(contribs, 'tgt', split_axis=0, concat_axis=0, tiled=True)  6.38 us
    dot_general x1, matrix products, per_device(): jnp.einsum('ctpi,pij->pctj', blocks, weights, preferred_element_type=jnp....  6.14 us
  transfers between devices with their start and end apart: 7, of which 4 were waited for; matrix products, arithmetic and copies ran while one was open for 13% of the time, Pallas kernels for 0%

commit v1 on v0

v1 whole, which is shorter than its diff:
```python
import jax
import jax.numpy as jnp
from jax import lax
from jax.experimental import pallas as pl
from jax.experimental.pallas import tpu as pltpu
from jax.sharding import PartitionSpec as P

BLK = 128
ID_ROWS = 16
W_CHUNK = 8
EOF_PARTS = 8
SHIFT = 64


def in_hbm(x):
    return pltpu.with_memory_space_constraint(x, pltpu.HBM)


def contribution_kernel(codes, vel_hbm, angle_ref, mirror_ref, w_hbm, out_hbm, vel, w, rot, out, vel_sem, w_sem, out_sem):
    components, rows, cells = vel.shape
    blocks = cells // BLK
    slots = w.shape[0]
    peers, peer_rows, _ = out.shape
    cap = slots // peers
    chunks = slots // W_CHUNK
    height = components * rows

    def w_copy(i):
        part = pl.ds(i * W_CHUNK, W_CHUNK)
        return pltpu.make_async_copy(w_hbm.at[part], w.at[part], w_sem.at[i])

    def out_copy(i):
        return pltpu.make_async_copy(out.at[i], out_hbm.at[i], out_sem.at[i])

    vel_copy = pltpu.make_async_copy(vel_hbm, vel, vel_sem)
    vel_copy.start()
    for i in range(chunks):
        w_copy(i).start()
    cosine = jnp.cos(angle_ref[...])
    sine = jnp.sin(angle_ref[...])
    lane = lax.broadcasted_iota(jnp.int32, (ID_ROWS, BLK), 1)
    for d in range(peers):
        ids = jnp.full((ID_ROWS, BLK), blocks, jnp.int32)
        for j in range(cap):
            ids = jnp.where(lane == j, codes[d * cap + j] % SHIFT, ids)
        out[d, cap * height :, :] = ids.astype(jnp.float32).astype(jnp.bfloat16)
    top = lax.axis_index("src") == lax.axis_size("src") - 1
    own_share = jnp.where(top, 0.5, 1.0).astype(jnp.float32)
    mirror_share = jnp.where(top, 0.5, 0.0).astype(jnp.float32)
    vel_copy.wait()
    for b in range(blocks):
        x = vel[0, :, b * BLK : (b + 1) * BLK].astype(jnp.float32)
        y = vel[1, :, b * BLK : (b + 1) * BLK].astype(jnp.float32)
        if b == blocks - 1:
            x = own_share * x - mirror_share * mirror_ref[0].astype(jnp.float32)
            y = own_share * y - mirror_share * mirror_ref[1].astype(jnp.float32)
        c = cosine[b : b + 1, :]
        s = sine[b : b + 1, :]
        rot[b, :rows, :] = (c * x - s * y).astype(jnp.bfloat16)
        rot[b, rows:, :] = (s * x + c * y).astype(jnp.bfloat16)

    for d in range(peers):
        for i in range(d * cap // W_CHUNK, (d + 1) * cap // W_CHUNK):
            w_copy(i).wait()
        for j in range(cap):
            p = d * cap + j
            block = rot[codes[p] // SHIFT]
            product = jnp.dot(block, w[p], preferred_element_type=jnp.float32)
            out[d, j * height : (j + 1) * height, :] = product.astype(jnp.bfloat16)
        out_copy(d).start()
    for d in range(peers):
        out_copy(d).wait()


def contributions(codes, src_vel, angle, mirror, weights, peers):
    components, rows, cells = src_vel.shape
    slots = weights.shape[0]
    blocks = cells // BLK
    height = components * rows
    peer_rows = slots // peers * height + ID_ROWS
    return pl.pallas_call(
        contribution_kernel,
        out_shape=jax.ShapeDtypeStruct((peers, peer_rows, BLK), jnp.bfloat16),
        in_specs=[
            pl.BlockSpec(memory_space=pltpu.SMEM),
            pl.BlockSpec(memory_space=pltpu.HBM),
            pl.BlockSpec(memory_space=pltpu.VMEM),
            pl.BlockSpec(memory_space=pltpu.VMEM),
            pl.BlockSpec(memory_space=pltpu.HBM),
        ],
        out_specs=pl.BlockSpec(memory_space=pltpu.HBM),
        scratch_shapes=[
            pltpu.VMEM(src_vel.shape, jnp.bfloat16),
            pltpu.VMEM(weights.shape, jnp.bfloat16),
            pltpu.VMEM((blocks, height, BLK), jnp.bfloat16),
            pltpu.VMEM((peers, peer_rows, BLK), jnp.bfloat16),
            pltpu.SemaphoreType.DMA,
            pltpu.SemaphoreType.DMA((slots // W_CHUNK,)),
            pltpu.SemaphoreType.DMA((peers,)),
        ],
        compiler_params=pltpu.CompilerParams(vmem_limit_bytes=24 << 20),
        name="contributions",
    )(codes, in_hbm(src_vel), angle.reshape(blocks, BLK), mirror, in_hbm(weights))


def remap_kernel(recv, eof_hbm, out_ref, pcs_ref, eof, acc, ids_vmem, ids_smem, sem, eof_sem):
    components, rows, cells = out_ref.shape
    blocks = cells // BLK
    peers, peer_rows, _ = recv.shape
    height = components * rows
    cap = (peer_rows - ID_ROWS) // height
    width = cells // EOF_PARTS

    def eof_copy(i):
        part = (slice(None), slice(None), pl.ds(i * width, width))
        return pltpu.make_async_copy(eof_hbm.at[part], eof.at[i], eof_sem.at[i])

    for i in range(EOF_PARTS):
        eof_copy(i).start()
    for s in range(peers):
        ids = recv[s, cap * height : cap * height + ID_ROWS, :].astype(jnp.float32).astype(jnp.int32)
        ids_vmem[s : s + 1, :] = ids[:1, :]
    copy = pltpu.make_async_copy(ids_vmem, ids_smem, sem)
    copy.start()
    acc[...] = jnp.zeros_like(acc)
    copy.wait()

    def sender(s, carry):
        for j in range(cap):
            start = pl.multiple_of(ids_smem[s, j] * height, height)
            part = recv[s, j * height : (j + 1) * height, :].astype(jnp.float32)
            acc[pl.ds(start, height), :] += part
        return carry

    lax.fori_loop(0, peers, sender, 0)
    for b in range(blocks):
        total = acc[b * height : (b + 1) * height, :].astype(jnp.bfloat16)
        for c in range(components):
            out_ref[c, :, b * BLK : (b + 1) * BLK] = total[c * rows : (c + 1) * rows, :]
    result = 0.0
    for i in range(EOF_PARTS):
        eof_copy(i).wait()
        for c in range(components):
            result += lax.dot_general(
                eof[i, c],
                out_ref[c, :, i * width : (i + 1) * width],
                (((1,), (1,)), ((), ())),
                preferred_element_type=jnp.float32,
            )
    pcs_ref[...] = result


def remap(received, eofs, rows):
    components, modes, cells = eofs.shape
    peers = received.shape[0]
    height = components * rows
    return pl.pallas_call(
        remap_kernel,
        out_shape=(
            jax.ShapeDtypeStruct((components, rows, cells), jnp.bfloat16),
            jax.ShapeDtypeStruct((modes, rows), jnp.float32),
        ),
        in_specs=[pl.BlockSpec(memory_space=pltpu.VMEM), pl.BlockSpec(memory_space=pltpu.HBM)],
        out_specs=(pl.BlockSpec(memory_space=pltpu.VMEM),) * 2,
        scratch_shapes=[
            pltpu.VMEM((EOF_PARTS, components, modes, cells // EOF_PARTS), jnp.bfloat16),
            pltpu.VMEM(((cells // BLK + 1) * height, BLK), jnp.float32),
            pltpu.VMEM((peers, BLK), jnp.int32),
            pltpu.SMEM((peers, BLK), jnp.int32),
            pltpu.SemaphoreType.DMA,
            pltpu.SemaphoreType.DMA((EOF_PARTS,)),
        ],
        compiler_params=pltpu.CompilerParams(vmem_limit_bytes=32 << 20),
        name="remap",
    )(received, in_hbm(eofs))


def per_device(src_vel, angle, src_block, tgt_block, send_count, intersection, eofs):
    components, rows, cells = src_vel.shape
    src_count = lax.axis_size("src")
    tgt_count = lax.axis_size("tgt")
    cap = src_block.shape[3]
    slots = tgt_count * cap
    blocks = eofs.shape[2] // BLK
    edge = src_vel[:, :, cells - BLK :][:, :, ::-1]
    top = (src_count - 1) * tgt_count
    mirror = lax.ppermute(
        edge, ("src", "tgt"), [(top + t, top + tgt_count - 1 - t) for t in range(tgt_count)]
    )
    live = lax.broadcasted_iota(jnp.int32, (1, 1, tgt_count, cap), 3) < send_count[..., None]
    codes = (src_block * SHIFT + jnp.where(live, tgt_block, blocks)).reshape(slots)
    weights = intersection.reshape(slots, BLK, BLK)
    contribs = contributions(codes, src_vel, angle, mirror, weights, tgt_count)
    received = lax.all_to_all(contribs, "tgt", split_axis=0, concat_axis=0, tiled=True)
    remapped, partial = remap(received, jnp.swapaxes(eofs, 0, 1), rows)
    modes = partial.shape[0] // tgt_count
    pieces = partial.reshape(tgt_count, 2, modes // 2, rows)
    pieces = jnp.concatenate([pieces[:, 0], pieces[:, 1]], axis=-1)
    column = jnp.sum(lax.all_to_all(pieces, "tgt", 0, 0, tiled=True), axis=0)
    everyone = jnp.broadcast_to(column[None], (src_count, *column.shape))
    total = jnp.sum(lax.all_to_all(everyone, "src", 0, 0, tiled=True), axis=0)
    pcs = jnp.concatenate([total[:, :rows], total[:, rows:]], axis=0).T
    return remapped, pcs


def solution(mesh):
    return jax.shard_map(
        per_device,
        mesh=mesh,
        in_specs=(
            P(None, None, ("src", "tgt")),
            P(("src", "tgt")),
            P("src", "tgt", None, None),
            P("src", "tgt", None, None),
            P("src", "tgt", None),
            P("src", "tgt", None, None, None, None),
            P(None, None, ("src", "tgt")),
        ),
        out_specs=(P(None, None, ("src", "tgt")), P(None, "tgt")),
        check_vma=False,
    )
```

time: 120 us -> 98.6 us (0.82)
  starting transfers between devices: 29.9 us -> 9.09 us
  matrix products: 16.2 us -> 0 us
  Pallas kernels: 0 us -> 14.3 us
  blocking collectives: 16 us -> 23.2 us
  waiting for transfers between devices: 40.6 us -> 35 us
  other arithmetic: 5.23 us -> 1.46 us
  local copies, waits for them, and re-layouts: 11 us -> 14.4 us
    dot_general x3 -> x0, matrix products: 16.2 us -> none  [the longest x1 8 us: per_device(): jnp.einsum('ctn,kcn->tk', remapped, eofs, preferred_element_type=jnp.floa...]
    pallas_call x0 -> x2, Pallas kernels: none -> 14.3 us  [the longest x1 7.52 us: contributions(): pl.pallas_call(contribution_kernel, out_shape=jax.ShapeDtypeStruct((peers...]
    all_to_all x2 -> x0, starting transfers between devices: 14.1 us -> none  [the longest x1 7.3 us: per_device(): lax.all_to_all(slot_ids, 'tgt', split_axis=0, concat_axis=0, tiled=True)]
    unnamed x8 -> x3, local copies, waits for them, and re-layouts: 2.04 us -> 13.3 us
    ppermute x4 -> x1, starting transfers between devices: 9.45 us -> 0.65 us  [per_device(): lax.ppermute(edge, ('src', 'tgt'), [(top + t, top + tgt_count - 1 - t) fo...]
    all_to_all x1 -> x2, blocking collectives: 16 us -> 23.2 us  [the longest x1 12.4 us: per_device(): total = jnp.sum(lax.all_to_all(everyone, 'src', 0, 0, tiled=True), axis=0)]
    all_to_all x2 -> x0, waiting for transfers between devices: 3.57 us -> none  [the longest x1 3.57 us: copy_for_each(): lax.all_to_all(jnp.broadcast_to(x[None], (size, *x.shape)), axis, 0, 0, t...]
    gather x1 -> x0, local copies, waits for them, and re-layouts: 2.63 us -> none  [per_device(): blocks = jnp.take(rotated, src_block.reshape(slot_total), axis=2)]
  transfers between devices with their start and end apart: 7 -> 2, of which waited for: 4 -> 1; matrix products, arithmetic and copies ran while one was open for 13% -> 14% of each run, Pallas kernels for 0% -> 0%
where the time goes in v1:
time: 98.6 us; the launch traced here: 98.1 us
  waiting for transfers between devices  35 us (35%)
  blocking collectives  23.2 us (24%)
  local copies, waits for them, and re-layouts  14.4 us (15%)
  Pallas kernels  14.3 us (15%)
  starting transfers between devices  9.09 us (9%)
  other arithmetic  1.46 us (1%)
    all_to_all x1, waiting for transfers between devices, per_device(): lax.all_to_all(contribs, 'tgt', split_axis=0, concat_axis=0, tiled=True)  35 us
    unnamed x3, local copies, waits for them, and re-layouts  13.3 us
    all_to_all x1, blocking collectives, per_device(): total = jnp.sum(lax.all_to_all(everyone, 'src', 0, 0, tiled=True), axis=0)  12.4 us
    all_to_all x1, blocking collectives, per_device(): column = jnp.sum(lax.all_to_all(pieces, 'tgt', 0, 0, tiled=True), axis=0)  10.8 us
    all_to_all x1, starting transfers between devices, per_device(): lax.all_to_all(contribs, 'tgt', split_axis=0, concat_axis=0, tiled=True)  8.44 us
    pallas_call x1, Pallas kernels, contributions(): pl.pallas_call(contribution_kernel, out_shape=jax.ShapeDtypeStruct((peers...  7.52 us
    pallas_call x1, Pallas kernels, remap(): pl.pallas_call(remap_kernel, out_shape=(jax.ShapeDtypeStruct((components,...  6.77 us
  transfers between devices with their start and end apart: 2, of which 1 were waited for; matrix products, arithmetic and copies ran while one was open for 14% of the time, Pallas kernels for 0%

profile of v1, /device:TPU:1, one launch (start us, length us, event | category | flops | bytes accessed | tf_op | source)
XLA Modules:
  0.0 98.1 jit_solution(6203095662589534097)
XLA Ops:
  0.6 0.7 slice.15
  1.4 0.1 rev.3
  1.5 0.7 collective-permute-start
  2.1 0.7 select_add_fusion
  2.8 0.1 copy.15
  2.9 0.1 reshape.52.codes
  3.0 0.0 collective-permute-done.mirror_ref
  3.0 0.0 copy-start
  3.0 0.7 copy-done
  3.7 7.5 %contributions.1 = bf16[16,784,128]{2,1,0:T(8,128)(2,1)} custom-call(s32[128]{0:T(128)S(1)} %reshape.52.codes, bf16[2,48,4096]{2,1,0:T(8,128)(2,1)} %vel_hbm.1, f32[32,128]{1,0:T(8,128)S(1)} %bitcast.18, bf16[2,48,128]{2,1,0:T(8,128)(2,1)S(1)} %collective-permute-done.mirror_ref, bf16[128,128,128]{2,1,0:T(8,128)(2,1)} %bitcast.20), custom_call_target="tpu_custom_call" | custom-call | tf_op jit(solution)/shard_map/contributions/pallas_call | solution.py:81
  11.3 8.4 %all-to-all-start = ((bf16[16,784,128]{2,1,0:T(8,128)(2,1)}), bf16[16,784,128]{2,1,0:T(8,128)(2,1)S(1)}, u32[]{:S(2)}, u32[]{:S(2)}) async-start(bf16[16,784,128]{2,1,0:T(8,128)(2,1)} %contributions.1), calls=%async_computation | async-start | bytes 6422528 | tf_op jit(solution)/shard_map/all_to_all | solution.py:194
  19.7 12.6 %copy.20 = bf16[512,2,4096]{2,0,1:T(8,128)(2,1)} copy(bf16[512,2,4096]{2,1,0:T(2,128)(2,1)} %param.13) | data formatting | bytes 16777216 | tf_op args[6]
  32.3 35.0 %all-to-all-done.recv = bf16[16,784,128]{2,1,0:T(8,128)(2,1)S(1)} async-done(((bf16[16,784,128]{2,1,0:T(8,128)(2,1)}), bf16[16,784,128]{2,1,0:T(8,128)(2,1)S(1)}, u32[]{:S(2)}, u32[]{:S(2)}) %all-to-all-start) | async-done | bytes 3211296 | tf_op jit(solution)/shard_map/all_to_all | solution.py:194
  67.3 6.8 %remap.1 = (bf16[2,48,4096]{2,1,0:T(8,128)(2,1)}, f32[512,48]{1,0:T(8,128)S(1)}) custom-call(bf16[16,784,128]{2,1,0:T(8,128)(2,1)S(1)} %all-to-all-done.recv, bf16[2,512,4096]{2,1,0:T(8,128)(2,1)} %bitcast.19), custom_call_target="tpu_custom_call" | custom-call | tf_op jit(solution)/shard_map/remap/pallas_call | solution.py:157
  74.1 0.1 pad_maximum_fusion
  74.2 10.8 %all_to_all.15 = f32[16,16,96]{2,1,0:T(8,128)S(1)} all-to-all(f32[16,16,96]{2,1,0:T(8,128)S(1)} %pad_maximum_fusion), channel_id=1, replica_groups=mesh['src'=8,'tgt'=16] {'tgt'}, dimensions={0} | all-to-all | bytes 196608 | tf_op jit(solution)/shard_map/all_to_all | solution.py:199
  85.1 12.4 %all_to_all.16 = f32[8,16,96]{2,1,0:T(8,128)S(1)} all-to-all(f32[8,16,96]{2,1,0:T(8,128)S(1)} %broadcast_in_dim.12), channel_id=1, replica_groups=mesh['src'=8,'tgt'=16] {'src'}, dimensions={0} | all-to-all | bytes 98304 | tf_op jit(solution)/shard_map/all_to_all | solution.py:201
  97.4 0.1 fusion
  97.5 0.6 maximum_bitcast_fusion
  (4 shorter events, 0.1 us)
Async XLA Ops:
  1.5 1.5 %collective-permute-start = (bf16[2,48,128]{2,1,0:T(8,128)(2,1)S(1)}, bf16[2,48,128]{2,1,0:T(8,128)(2,1)S(1)}, u32[]{:S(2)}, u32[]{:S(2)}) collective-permute-start(bf16[2,48,128]{2,1,0:T(8,128)(2,1)S(1)} %rev.3), channel_id=1, source_target_pairs={{112,127},{113,126},{114,125},{115,124},{116,123},{117,122},{118,1... | collective-permute-start | bytes 73736 | tf_op jit(solution)/shard_map/ppermute | solution.py:187
  3.0 0.7 copy-start
  11.3 56.1 %all-to-all-start = ((bf16[16,784,128]{2,1,0:T(8,128)(2,1)}), bf16[16,784,128]{2,1,0:T(8,128)(2,1)S(1)}, u32[]{:S(2)}, u32[]{:S(2)}) async-start(bf16[16,784,128]{2,1,0:T(8,128)(2,1)} %contributions.1), calls=%async_computation | async-start | bytes 6422528 | tf_op jit(solution)/shard_map/all_to_all | solution.py:194

commit v2 on v1

v2 whole, which is shorter than its diff:
```python
import jax
import jax.numpy as jnp
from jax import lax
from jax.experimental import pallas as pl
from jax.experimental.pallas import tpu as pltpu
from jax.sharding import PartitionSpec as P

BLK = 128
ID_ROWS = 16
W_CHUNK = 8
EOF_PARTS = 2


def in_hbm(x):
    return pltpu.with_memory_space_constraint(x, pltpu.HBM)


def contribution_kernel(src_ids, tgt_ids, counts, vel_hbm, angle_hbm, mirror_ref, w_hbm, out, vel, angle, w, rot, vel_sem, angle_sem, w_sem):
    components, rows, cells = vel.shape
    blocks = cells // BLK
    slots = w.shape[0]
    peers, peer_rows, _ = out.shape
    cap = slots // peers
    chunks = slots // W_CHUNK
    height = components * rows

    def w_copy(i):
        part = pl.ds(i * W_CHUNK, W_CHUNK)
        return pltpu.make_async_copy(w_hbm.at[part], w.at[part], w_sem.at[i])

    angle_copy = pltpu.make_async_copy(angle_hbm, angle, angle_sem)
    angle_copy.start()
    vel_copy = pltpu.make_async_copy(vel_hbm, vel, vel_sem)
    vel_copy.start()
    for i in range(chunks):
        w_copy(i).start()
    lane = lax.broadcasted_iota(jnp.int32, (ID_ROWS, BLK), 1)
    for d in range(peers):
        ids = jnp.full((ID_ROWS, BLK), blocks, jnp.int32)
        for j in range(cap):
            ids = jnp.where(lane == j, jnp.where(j < counts[d], tgt_ids[j, d], blocks), ids)
        out[d, cap * height :, :] = ids.astype(jnp.float32).astype(jnp.bfloat16)
    top = lax.axis_index("src") == lax.axis_size("src") - 1
    own_share = jnp.where(top, 0.5, 1.0).astype(jnp.float32)
    mirror_share = jnp.where(top, 0.5, 0.0).astype(jnp.float32)
    angle_copy.wait()
    cosine = jnp.cos(angle[...])
    sine = jnp.sin(angle[...])
    vel_copy.wait()
    for b in range(blocks):
        x = vel[0, :, b * BLK : (b + 1) * BLK].astype(jnp.float32)
        y = vel[1, :, b * BLK : (b + 1) * BLK].astype(jnp.float32)
        if b == blocks - 1:
            x = own_share * x - mirror_share * mirror_ref[0].astype(jnp.float32)
            y = own_share * y - mirror_share * mirror_ref[1].astype(jnp.float32)
        c = cosine[b : b + 1, :]
        s = sine[b : b + 1, :]
        rot[b, :rows, :] = (c * x - s * y).astype(jnp.bfloat16)
        rot[b, rows:, :] = (s * x + c * y).astype(jnp.bfloat16)

    for d in range(peers):
        for i in range(d * cap // W_CHUNK, (d + 1) * cap // W_CHUNK):
            w_copy(i).wait()
        for j in range(cap):
            p = d * cap + j
            block = rot[src_ids[j, d]]
            product = jnp.dot(block, w[p], preferred_element_type=jnp.float32)
            out[d, j * height : (j + 1) * height, :] = product.astype(jnp.bfloat16)


def contributions(src_ids, tgt_ids, counts, src_vel, angle, mirror, weights, peers):
    components, rows, cells = src_vel.shape
    slots = weights.shape[0]
    blocks = cells // BLK
    height = components * rows
    peer_rows = slots // peers * height + ID_ROWS
    return pl.pallas_call(
        contribution_kernel,
        out_shape=jax.ShapeDtypeStruct((peers, peer_rows, BLK), jnp.bfloat16),
        in_specs=[
            pl.BlockSpec(memory_space=pltpu.SMEM),
            pl.BlockSpec(memory_space=pltpu.SMEM),
            pl.BlockSpec(memory_space=pltpu.SMEM),
            pl.BlockSpec(memory_space=pltpu.HBM),
            pl.BlockSpec(memory_space=pltpu.HBM),
            pl.BlockSpec(memory_space=pltpu.VMEM),
            pl.BlockSpec(memory_space=pltpu.HBM),
        ],
        out_specs=pl.BlockSpec(memory_space=pltpu.VMEM),
        scratch_shapes=[
            pltpu.VMEM(src_vel.shape, jnp.bfloat16),
            pltpu.VMEM((blocks, BLK), jnp.float32),
            pltpu.VMEM(weights.shape, jnp.bfloat16),
            pltpu.VMEM((blocks, height, BLK), jnp.bfloat16),
            pltpu.SemaphoreType.DMA,
            pltpu.SemaphoreType.DMA,
            pltpu.SemaphoreType.DMA((slots // W_CHUNK,)),
        ],
        compiler_params=pltpu.CompilerParams(vmem_limit_bytes=24 << 20),
        name="contributions",
    )(in_hbm(src_ids), in_hbm(tgt_ids), in_hbm(counts), in_hbm(src_vel), in_hbm(angle.reshape(blocks, BLK)), mirror, in_hbm(weights))


def remap_kernel(recv, eof_ref, out_ref, pcs_ref, eof, acc, ids_vmem, ids_smem, sem):
    components, rows, cells = out_ref.shape
    blocks = cells // BLK
    peers, peer_rows, _ = recv.shape
    height = components * rows
    cap = (peer_rows - ID_ROWS) // height
    for s in range(peers):
        ids = recv[s, cap * height : cap * height + ID_ROWS, :].astype(jnp.float32).astype(jnp.int32)
        ids_vmem[s : s + 1, :] = ids[:1, :]
    copy = pltpu.make_async_copy(ids_vmem, ids_smem, sem)
    copy.start()
    acc[...] = jnp.zeros_like(acc)
    copy.wait()

    def sender(s, carry):
        for j in range(cap):
            start = pl.multiple_of(ids_smem[s, j] * height, height)
            part = recv[s, j * height : (j + 1) * height, :].astype(jnp.float32)
            acc[pl.ds(start, height), :] += part
        return carry

    lax.fori_loop(0, peers, sender, 0)
    for b in range(blocks):
        total = acc[b * height : (b + 1) * height, :].astype(jnp.bfloat16)
        for c in range(components):
            out_ref[c, :, b * BLK : (b + 1) * BLK] = total[c * rows : (c + 1) * rows, :]
    modes = eof_ref.shape[0]
    width = modes // EOF_PARTS
    half = pcs_ref.shape[1]
    pcs_ref[...] = jnp.zeros_like(pcs_ref)
    for i in range(EOF_PARTS):
        eof[i] = jnp.swapaxes(eof_ref[i * width : (i + 1) * width], 0, 1)
        result = 0.0
        for c in range(components):
            result += lax.dot_general(
                out_ref[c], eof[i, c], (((1,), (1,)), ((), ())), preferred_element_type=jnp.float32
            )
        pieces = result.T.reshape(width // (2 * half), 2 * half, rows)
        first = i * width // (2 * half)
        pcs_ref[first : first + width // (2 * half), :, :rows] = pieces[:, :half]
        pcs_ref[first : first + width // (2 * half), :, BLK // 2 : BLK // 2 + rows] = pieces[:, half:]


def remap(received, eofs, rows):
    modes, components, cells = eofs.shape
    peers = received.shape[0]
    height = components * rows
    return pl.pallas_call(
        remap_kernel,
        out_shape=(
            jax.ShapeDtypeStruct((components, rows, cells), jnp.bfloat16),
            jax.ShapeDtypeStruct((peers, modes // peers // 2, BLK), jnp.float32),
        ),
        in_specs=[pl.BlockSpec(memory_space=pltpu.VMEM)] * 2,
        out_specs=(pl.BlockSpec(memory_space=pltpu.VMEM),) * 2,
        scratch_shapes=[
            pltpu.VMEM((EOF_PARTS, components, modes // EOF_PARTS, cells), jnp.bfloat16),
            pltpu.VMEM(((cells // BLK + 1) * height, BLK), jnp.float32),
            pltpu.VMEM((peers, BLK), jnp.int32),
            pltpu.SMEM((peers, BLK), jnp.int32),
            pltpu.SemaphoreType.DMA,
        ],
        compiler_params=pltpu.CompilerParams(vmem_limit_bytes=32 << 20),
        name="remap",
    )(received, eofs)


def per_device(src_vel, angle, src_block, tgt_block, send_count, intersection, eofs):
    components, rows, cells = src_vel.shape
    src_count = lax.axis_size("src")
    tgt_count = lax.axis_size("tgt")
    cap = src_block.shape[3]
    slots = tgt_count * cap
    blocks = eofs.shape[2] // BLK
    edge = src_vel[:, :, cells - BLK :][:, :, ::-1]
    top = (src_count - 1) * tgt_count
    mirror = lax.ppermute(
        edge, ("src", "tgt"), [(top + t, top + tgt_count - 1 - t) for t in range(tgt_count)]
    )
    src_ids = jnp.swapaxes(src_block, 2, 3).reshape(cap, tgt_count)
    tgt_ids = jnp.swapaxes(tgt_block, 2, 3).reshape(cap, tgt_count)
    counts = send_count.reshape(tgt_count)
    weights = intersection.reshape(slots, BLK, BLK)
    contribs = contributions(
        src_ids, tgt_ids, counts, src_vel, angle, mirror, weights, tgt_count
    )
    contribs, eofs = lax.optimization_barrier((contribs, eofs))
    received = lax.all_to_all(contribs, "tgt", split_axis=0, concat_axis=0, tiled=True)
    remapped, partial = remap(received, eofs, rows)
    column = jnp.sum(lax.all_to_all(partial, "tgt", 0, 0, tiled=True), axis=0)
    everyone = jnp.broadcast_to(column[None], (src_count, *column.shape))
    total = jnp.sum(lax.all_to_all(everyone, "src", 0, 0, tiled=True), axis=0)
    pcs = jnp.concatenate([total[:, :rows], total[:, BLK // 2 : BLK // 2 + rows]], axis=0).T
    return remapped, pcs


def solution(mesh):
    return jax.shard_map(
        per_device,
        mesh=mesh,
        in_specs=(
            P(None, None, ("src", "tgt")),
            P(("src", "tgt")),
            P("src", "tgt", None, None),
            P("src", "tgt", None, None),
            P("src", "tgt", None),
            P("src", "tgt", None, None, None, None),
            P(None, None, ("src", "tgt")),
        ),
        out_specs=(P(None, None, ("src", "tgt")), P(None, "tgt")),
        check_vma=False,
    )
```

time: 98.6 us -> 87.8 us (0.89)
  blocking collectives: 23.2 us -> 70.5 us
  waiting for transfers between devices: 35 us -> 0.01 us
  local copies, waits for them, and re-layouts: 14.4 us -> 0.92 us
  starting transfers between devices: 9.09 us -> 0.65 us
    all_to_all x1 -> x2, blocking collectives: 10.8 us -> 57.4 us  [the longest x1 47.6 us: per_device(): lax.all_to_all(contribs, 'tgt', split_axis=0, concat_axis=0, tiled=True)]
    all_to_all x1 -> x0, waiting for transfers between devices: 35 us -> none  [per_device(): lax.all_to_all(contribs, 'tgt', split_axis=0, concat_axis=0, tiled=True)]
    unnamed x3 -> x2, local copies, waits for them, and re-layouts: 13.3 us -> 0.01 us
    all_to_all x1 -> x0, starting transfers between devices: 8.44 us -> none  [per_device(): lax.all_to_all(contribs, 'tgt', split_axis=0, concat_axis=0, tiled=True)]
  transfers between devices with their start and end apart: 2 -> 1, of which waited for: 1 -> 0; matrix products, arithmetic and copies ran while one was open for 14% -> 0% of each run, Pallas kernels for 0% -> 0%
where the time goes in v2:
time: 87.8 us; the launch traced here: 87.6 us
  blocking collectives  70.5 us (80%)
  Pallas kernels  14.2 us (16%)
  local copies, waits for them, and re-layouts  0.92 us (1%)
    all_to_all x1, blocking collectives, per_device(): lax.all_to_all(contribs, 'tgt', split_axis=0, concat_axis=0, tiled=True)  47.6 us
    all_to_all x1, blocking collectives, per_device(): total = jnp.sum(lax.all_to_all(everyone, 'src', 0, 0, tiled=True), axis=0)  13.1 us
    all_to_all x1, blocking collectives, per_device(): column = jnp.sum(lax.all_to_all(partial, 'tgt', 0, 0, tiled=True), axis=0)  9.84 us
    pallas_call x1, Pallas kernels, contributions(): pl.pallas_call(contribution_kernel, out_shape=jax.ShapeDtypeStruct((peers...  7.54 us
    pallas_call x1, Pallas kernels, remap(): pl.pallas_call(remap_kernel, out_shape=(jax.ShapeDtypeStruct((components,...  6.64 us
  transfers between devices with their start and end apart: 1, of which 0 were waited for; matrix products, arithmetic and copies ran while one was open for 0% of the time, Pallas kernels for 0%

profile of v2, /device:TPU:1, one launch (start us, length us, event | category | flops | bytes accessed | tf_op | source)
XLA Modules:
  0.0 87.6 jit_solution(10348099090337545166)
XLA Ops:
  0.6 0.7 slice.9
  1.4 0.1 rev.3
  1.5 0.7 collective-permute-start
  2.1 0.0 collective-permute-done.mirror_ref
  2.1 0.0 copy-start
  2.1 7.5 %contributions.1 = bf16[16,784,128]{2,1,0:T(8,128)(2,1)S(1)} custom-call(s32[8,16]{1,0:T(8,128)} %bitcast.13, s32[8,16]{1,0:T(8,128)} %bitcast.14, s32[16]{0:T(128)} %bitcast.15, bf16[2,48,4096]{2,1,0:T(8,128)(2,1)} %vel_hbm.1, f32[32,128]{1,0:T(8,128)} %bitcast.12, bf16[2,48,128]{2,1,0:T(8,128)(2,1)S(1)} %collective-permute-done.mirror_ref, ...), custom_call_target="tpu_custom_call" | custom-call | tf_op jit(solution)/shard_map/contributions/pallas_call | solution.py:77
  9.7 47.6 %all_to_all.15.recv = bf16[16,784,128]{2,1,0:T(8,128)(2,1)S(1)} all-to-all(bf16[16,784,128]{2,1,0:T(8,128)(2,1)S(1)} %contributions.1), channel_id=1, replica_groups=mesh['src'=8,'tgt'=16] {'tgt'}, dimensions={0} | all-to-all | bytes 6422528 | tf_op jit(solution)/shard_map/all_to_all | solution.py:191
  57.3 0.0 copy-done
  57.3 6.6 %remap.1 = (bf16[2,48,4096]{2,1,0:T(8,128)(2,1)}, f32[16,16,128]{2,1,0:T(8,128)S(1)}) custom-call(bf16[16,784,128]{2,1,0:T(8,128)(2,1)S(1)} %all_to_all.15.recv, bf16[512,2,4096]{2,1,0:T(2,128)(2,1)S(1)} %copy-done), custom_call_target="tpu_custom_call" | custom-call | tf_op jit(solution)/shard_map/remap/pallas_call | solution.py:151
  63.9 9.8 %all_to_all.16 = f32[16,16,128]{2,1,0:T(8,128)S(1)} all-to-all(f32[16,16,128]{2,1,0:T(8,128)S(1)} %get-tuple-element.9), channel_id=1, replica_groups=mesh['src'=8,'tgt'=16] {'tgt'}, dimensions={0} | all-to-all | bytes 262144 | tf_op jit(solution)/shard_map/all_to_all | solution.py:193
  73.8 13.1 %all_to_all.17 = f32[8,16,128]{2,1,0:T(8,128)S(1)} all-to-all(f32[8,16,128]{2,1,0:T(8,128)S(1)} %broadcast_in_dim.2), channel_id=1, replica_groups=mesh['src'=8,'tgt'=16] {'src'}, dimensions={0} | all-to-all | bytes 131072 | tf_op jit(solution)/shard_map/all_to_all | solution.py:195
  86.9 0.1 fusion
  87.0 0.6 maximum_bitcast_fusion
  (3 shorter events, 0.0 us)
Async XLA Ops:
  1.5 0.7 collective-permute-start
  2.1 55.1 %copy-start = (bf16[512,2,4096]{2,1,0:T(2,128)(2,1)S(1)}, bf16[512,2,4096]{2,1,0:T(2,128)(2,1)}, u32[]{:S(2)}) copy-start(bf16[512,2,4096]{2,1,0:T(2,128)(2,1)} %eof_ref) | copy-start | bytes 25165828

commit v3 on v2

--- a/solution.py
+++ b/solution.py
@@ -7,7 +7,7 @@
 
 BLK = 128
 ID_ROWS = 16
-W_CHUNK = 8
+W_CHUNK = 64
 EOF_PARTS = 2
 
 
@@ -59,8 +59,8 @@
         rot[b, rows:, :] = (s * x + c * y).astype(jnp.bfloat16)
 
     for d in range(peers):
-        for i in range(d * cap // W_CHUNK, (d + 1) * cap // W_CHUNK):
-            w_copy(i).wait()
+        if d * cap % W_CHUNK == 0:
+            w_copy(d * cap // W_CHUNK).wait()
         for j in range(cap):
             p = d * cap + j
             block = rot[src_ids[j, d]]
@@ -101,7 +101,7 @@
     )(in_hbm(src_ids), in_hbm(tgt_ids), in_hbm(counts), in_hbm(src_vel), in_hbm(angle.reshape(blocks, BLK)), mirror, in_hbm(weights))
 
 
-def remap_kernel(recv, eof_ref, out_ref, pcs_ref, eof, acc, ids_vmem, ids_smem, sem):
+def remap_kernel(recv, eof_ref, out_ref, pcs_ref, eof, mixed, acc, ids_vmem, ids_smem, sem):
     components, rows, cells = out_ref.shape
     blocks = cells // BLK
     peers, peer_rows, _ = recv.shape
@@ -112,7 +112,11 @@
         ids_vmem[s : s + 1, :] = ids[:1, :]
     copy = pltpu.make_async_copy(ids_vmem, ids_smem, sem)
     copy.start()
+    modes = eof_ref.shape[0]
+    width = modes // EOF_PARTS
     acc[...] = jnp.zeros_like(acc)
+    for i in range(EOF_PARTS):
+        eof[i] = eof_ref[i * width : (i + 1) * width].reshape(components * width, cells)
     copy.wait()
 
     def sender(s, carry):
@@ -132,13 +136,17 @@
     half = pcs_ref.shape[1]
     pcs_ref[...] = jnp.zeros_like(pcs_ref)
     for i in range(EOF_PARTS):
-        eof[i] = jnp.swapaxes(eof_ref[i * width : (i + 1) * width], 0, 1)
+        product = lax.dot_general(
+            out_ref[...].reshape(height, cells),
+            eof[i],
+            (((1,), (1,)), ((), ())),
+            preferred_element_type=jnp.float32,
+        )
+        mixed[:, :height] = product.T
         result = 0.0
         for c in range(components):
-            result += lax.dot_general(
-                out_ref[c], eof[i, c], (((1,), (1,)), ((), ())), preferred_element_type=jnp.float32
-            )
-        pieces = result.T.reshape(width // (2 * half), 2 * half, rows)
+            result += mixed[pl.ds(c, width, stride=components), :][:, c * rows : (c + 1) * rows]
+        pieces = result.reshape(width // (2 * half), 2 * half, rows)
         first = i * width // (2 * half)
         pcs_ref[first : first + width // (2 * half), :, :rows] = pieces[:, :half]
         pcs_ref[first : first + width // (2 * half), :, BLK // 2 : BLK // 2 + rows] = pieces[:, half:]
@@ -157,7 +165,8 @@
         in_specs=[pl.BlockSpec(memory_space=pltpu.VMEM)] * 2,
         out_specs=(pl.BlockSpec(memory_space=pltpu.VMEM),) * 2,
         scratch_shapes=[
-            pltpu.VMEM((EOF_PARTS, components, modes // EOF_PARTS, cells), jnp.bfloat16),
+            pltpu.VMEM((EOF_PARTS, components * modes // EOF_PARTS, cells), jnp.bfloat16),
+            pltpu.VMEM((components * modes // EOF_PARTS, BLK), jnp.float32),
             pltpu.VMEM(((cells // BLK + 1) * height, BLK), jnp.float32),
             pltpu.VMEM((peers, BLK), jnp.int32),
             pltpu.SMEM((peers, BLK), jnp.int32),

time: 87.8 us -> 83.5 us (0.951)
  Pallas kernels: 14.2 us -> 9.83 us
    pallas_call x1, Pallas kernels: 7.54 us -> 4.77 us  [contributions(): pl.pallas_call(contribution_kernel, out_shape=jax.ShapeDtypeStruct((peers...]
    pallas_call x1, Pallas kernels: 6.64 us -> 5.06 us  [remap(): pl.pallas_call(remap_kernel, out_shape=(jax.ShapeDtypeStruct((components,...]
where the time goes in v3:
time: 83.5 us; the launch traced here: 83.2 us
  blocking collectives  70.5 us (84%)
  Pallas kernels  9.83 us (12%)
  local copies, waits for them, and re-layouts  0.92 us (1%)
    all_to_all x1, blocking collectives, per_device(): lax.all_to_all(contribs, 'tgt', split_axis=0, concat_axis=0, tiled=True)  47.6 us
    all_to_all x1, blocking collectives, per_device(): total = jnp.sum(lax.all_to_all(everyone, 'src', 0, 0, tiled=True), axis=0)  13.1 us
    all_to_all x1, blocking collectives, per_device(): column = jnp.sum(lax.all_to_all(partial, 'tgt', 0, 0, tiled=True), axis=0)  9.82 us
    pallas_call x1, Pallas kernels, remap(): pl.pallas_call(remap_kernel, out_shape=(jax.ShapeDtypeStruct((components,...  5.06 us
    pallas_call x1, Pallas kernels, contributions(): pl.pallas_call(contribution_kernel, out_shape=jax.ShapeDtypeStruct((peers...  4.77 us
  transfers between devices with their start and end apart: 1, of which 0 were waited for; matrix products, arithmetic and copies ran while one was open for 0% of the time, Pallas kernels for 0%

profile of v3, /device:TPU:1, one launch (start us, length us, event | category | flops | bytes accessed | tf_op | source)
XLA Modules:
  0.0 83.2 jit_solution(9874401513284269939)
XLA Ops:
  0.6 0.7 slice.9
  1.4 0.1 rev.3
  1.5 0.7 collective-permute-start
  2.1 0.0 collective-permute-done.mirror_ref
  2.1 0.0 copy-start
  2.1 4.8 %contributions.1 = bf16[16,784,128]{2,1,0:T(8,128)(2,1)S(1)} custom-call(s32[8,16]{1,0:T(8,128)} %bitcast.13, s32[8,16]{1,0:T(8,128)} %bitcast.14, s32[16]{0:T(128)} %bitcast.15, bf16[2,48,4096]{2,1,0:T(8,128)(2,1)} %vel_hbm.1, f32[32,128]{1,0:T(8,128)} %bitcast.12, bf16[2,48,128]{2,1,0:T(8,128)(2,1)S(1)} %collective-permute-done.mirror_ref, ...), custom_call_target="tpu_custom_call" | custom-call | tf_op jit(solution)/shard_map/contributions/pallas_call | solution.py:77
  6.9 47.6 %all_to_all.15.recv = bf16[16,784,128]{2,1,0:T(8,128)(2,1)S(1)} all-to-all(bf16[16,784,128]{2,1,0:T(8,128)(2,1)S(1)} %contributions.1), channel_id=1, replica_groups=mesh['src'=8,'tgt'=16] {'tgt'}, dimensions={0} | all-to-all | bytes 6422528 | tf_op jit(solution)/shard_map/all_to_all | solution.py:200
  54.5 0.0 copy-done
  54.5 5.1 %remap.1 = (bf16[2,48,4096]{2,1,0:T(8,128)(2,1)}, f32[16,16,128]{2,1,0:T(8,128)S(1)}) custom-call(bf16[16,784,128]{2,1,0:T(8,128)(2,1)S(1)} %all_to_all.15.recv, bf16[512,2,4096]{2,1,0:T(2,128)(2,1)S(1)} %copy-done), custom_call_target="tpu_custom_call" | custom-call | tf_op jit(solution)/shard_map/remap/pallas_call | solution.py:159
  59.6 9.8 %all_to_all.16 = f32[16,16,128]{2,1,0:T(8,128)S(1)} all-to-all(f32[16,16,128]{2,1,0:T(8,128)S(1)} %get-tuple-element.9), channel_id=1, replica_groups=mesh['src'=8,'tgt'=16] {'tgt'}, dimensions={0} | all-to-all | bytes 262144 | tf_op jit(solution)/shard_map/all_to_all | solution.py:202
  69.4 13.1 %all_to_all.17 = f32[8,16,128]{2,1,0:T(8,128)S(1)} all-to-all(f32[8,16,128]{2,1,0:T(8,128)S(1)} %broadcast_in_dim.2), channel_id=1, replica_groups=mesh['src'=8,'tgt'=16] {'src'}, dimensions={0} | all-to-all | bytes 131072 | tf_op jit(solution)/shard_map/all_to_all | solution.py:204
  82.6 0.1 fusion
  82.6 0.6 maximum_bitcast_fusion
  (3 shorter events, 0.0 us)
Async XLA Ops:
  1.5 0.7 collective-permute-start
  2.1 52.4 %copy-start = (bf16[512,2,4096]{2,1,0:T(2,128)(2,1)S(1)}, bf16[512,2,4096]{2,1,0:T(2,128)(2,1)}, u32[]{:S(2)}) copy-start(bf16[512,2,4096]{2,1,0:T(2,128)(2,1)} %eof_ref) | copy-start | bytes 25165828

commit v4 on v3

--- a/solution.py
+++ b/solution.py
@@ -6,7 +6,7 @@
 from jax.sharding import PartitionSpec as P
 
 BLK = 128
-ID_ROWS = 16
+ID_ROWS = 8
 W_CHUNK = 64
 EOF_PARTS = 2
 
@@ -15,7 +15,26 @@
     return pltpu.with_memory_space_constraint(x, pltpu.HBM)
 
 
-def contribution_kernel(src_ids, tgt_ids, counts, vel_hbm, angle_hbm, mirror_ref, w_hbm, out, vel, angle, w, rot, vel_sem, angle_sem, w_sem):
+def contribution_kernel(
+    src_ids_hbm,
+    tgt_ids_hbm,
+    counts_hbm,
+    vel_hbm,
+    angle_hbm,
+    w_hbm,
+    out,
+    w,
+    trig,
+    src_ids,
+    tgt_ids,
+    counts,
+    vel,
+    angle,
+    rot,
+    small_sem,
+    vel_sem,
+    w_sem,
+):
     components, rows, cells = vel.shape
     blocks = cells // BLK
     slots = w.shape[0]
@@ -28,31 +47,34 @@
         part = pl.ds(i * W_CHUNK, W_CHUNK)
         return pltpu.make_async_copy(w_hbm.at[part], w.at[part], w_sem.at[i])
 
-    angle_copy = pltpu.make_async_copy(angle_hbm, angle, angle_sem)
-    angle_copy.start()
+    small = [
+        pltpu.make_async_copy(src, dst, small_sem.at[i])
+        for i, (src, dst) in enumerate(
+            [(src_ids_hbm, src_ids), (tgt_ids_hbm, tgt_ids), (counts_hbm, counts), (angle_hbm, angle)]
+        )
+    ]
+    for copy in small:
+        copy.start()
     vel_copy = pltpu.make_async_copy(vel_hbm, vel, vel_sem)
     vel_copy.start()
     for i in range(chunks):
         w_copy(i).start()
+    for copy in small:
+        copy.wait()
     lane = lax.broadcasted_iota(jnp.int32, (ID_ROWS, BLK), 1)
     for d in range(peers):
         ids = jnp.full((ID_ROWS, BLK), blocks, jnp.int32)
         for j in range(cap):
             ids = jnp.where(lane == j, jnp.where(j < counts[d], tgt_ids[j, d], blocks), ids)
         out[d, cap * height :, :] = ids.astype(jnp.float32).astype(jnp.bfloat16)
-    top = lax.axis_index("src") == lax.axis_size("src") - 1
-    own_share = jnp.where(top, 0.5, 1.0).astype(jnp.float32)
-    mirror_share = jnp.where(top, 0.5, 0.0).astype(jnp.float32)
-    angle_copy.wait()
     cosine = jnp.cos(angle[...])
     sine = jnp.sin(angle[...])
+    trig[0] = cosine
+    trig[1] = sine
     vel_copy.wait()
     for b in range(blocks):
         x = vel[0, :, b * BLK : (b + 1) * BLK].astype(jnp.float32)
         y = vel[1, :, b * BLK : (b + 1) * BLK].astype(jnp.float32)
-        if b == blocks - 1:
-            x = own_share * x - mirror_share * mirror_ref[0].astype(jnp.float32)
-            y = own_share * y - mirror_share * mirror_ref[1].astype(jnp.float32)
         c = cosine[b : b + 1, :]
         s = sine[b : b + 1, :]
         rot[b, :rows, :] = (c * x - s * y).astype(jnp.bfloat16)
@@ -68,7 +90,7 @@
             out[d, j * height : (j + 1) * height, :] = product.astype(jnp.bfloat16)
 
 
-def contributions(src_ids, tgt_ids, counts, src_vel, angle, mirror, weights, peers):
+def contributions(src_ids, tgt_ids, counts, src_vel, angle, weights, peers):
     components, rows, cells = src_vel.shape
     slots = weights.shape[0]
     blocks = cells // BLK
@@ -76,29 +98,75 @@
     peer_rows = slots // peers * height + ID_ROWS
     return pl.pallas_call(
         contribution_kernel,
-        out_shape=jax.ShapeDtypeStruct((peers, peer_rows, BLK), jnp.bfloat16),
+        out_shape=(
+            jax.ShapeDtypeStruct((peers, peer_rows, BLK), jnp.bfloat16),
+            jax.ShapeDtypeStruct(weights.shape, jnp.bfloat16),
+            jax.ShapeDtypeStruct((2, blocks, BLK), jnp.float32),
+        ),
         in_specs=[
-            pl.BlockSpec(memory_space=pltpu.SMEM),
-            pl.BlockSpec(memory_space=pltpu.SMEM),
-            pl.BlockSpec(memory_space=pltpu.SMEM),
             pl.BlockSpec(memory_space=pltpu.HBM),
-            pl.BlockSpec(memory_space=pltpu.HBM),
-            pl.BlockSpec(memory_space=pltpu.VMEM),
-            pl.BlockSpec(memory_space=pltpu.HBM),
-        ],
-        out_specs=pl.BlockSpec(memory_space=pltpu.VMEM),
+        ]
+        * 6,
+        out_specs=(pl.BlockSpec(memory_space=pltpu.VMEM),) * 3,
         scratch_shapes=[
+            pltpu.SMEM(src_ids.shape, jnp.int32),
+            pltpu.SMEM(tgt_ids.shape, jnp.int32),
+            pltpu.SMEM(counts.shape, jnp.int32),
             pltpu.VMEM(src_vel.shape, jnp.bfloat16),
             pltpu.VMEM((blocks, BLK), jnp.float32),
-            pltpu.VMEM(weights.shape, jnp.bfloat16),
             pltpu.VMEM((blocks, height, BLK), jnp.bfloat16),
-            pltpu.SemaphoreType.DMA,
+            pltpu.SemaphoreType.DMA((4,)),
             pltpu.SemaphoreType.DMA,
             pltpu.SemaphoreType.DMA((slots // W_CHUNK,)),
         ],
         compiler_params=pltpu.CompilerParams(vmem_limit_bytes=24 << 20),
         name="contributions",
-    )(in_hbm(src_ids), in_hbm(tgt_ids), in_hbm(counts), in_hbm(src_vel), in_hbm(angle.reshape(blocks, BLK)), mirror, in_hbm(weights))
+    )(in_hbm(src_ids), in_hbm(tgt_ids), in_hbm(counts), in_hbm(src_vel), in_hbm(angle.reshape(blocks, BLK)), in_hbm(weights))
+
+
+def fold_kernel(given, w, trig, edge, mirror, ids_hbm, out, block, ids, sem):
+    _, rows, _ = edge.shape
+    blocks = trig.shape[1]
+    peers = out.shape[0]
+    cap = ids.shape[0]
+    height = block.shape[0]
+
+    @pl.when(lax.axis_index("src") == lax.axis_size("src") - 1)
+    def _():
+        copy = pltpu.make_async_copy(ids_hbm, ids, sem)
+        copy.start()
+        x = 0.5 * (edge[0].astype(jnp.float32) - mirror[0].astype(jnp.float32))
+        y = 0.5 * (edge[1].astype(jnp.float32) - mirror[1].astype(jnp.float32))
+        c = trig[0, blocks - 1 : blocks, :]
+        s = trig[1, blocks - 1 : blocks, :]
+        block[:rows, :] = (c * x - s * y).astype(jnp.bfloat16)
+        block[rows:, :] = (s * x + c * y).astype(jnp.bfloat16)
+        copy.wait()
+        for d in range(peers):
+            for j in range(cap):
+
+                @pl.when(ids[j, d] == blocks - 1)
+                def _():
+                    product = jnp.dot(block[...], w[d * cap + j], preferred_element_type=jnp.float32)
+                    out[d, j * height : (j + 1) * height, :] = product.astype(jnp.bfloat16)
+
+
+def fold(contribs, weights, trig, edge, mirror, src_ids):
+    components, rows, _ = edge.shape
+    return pl.pallas_call(
+        fold_kernel,
+        out_shape=jax.ShapeDtypeStruct(contribs.shape, contribs.dtype),
+        in_specs=[pl.BlockSpec(memory_space=pltpu.VMEM)] * 5 + [pl.BlockSpec(memory_space=pltpu.HBM)],
+        out_specs=pl.BlockSpec(memory_space=pltpu.VMEM),
+        scratch_shapes=[
+            pltpu.VMEM((components * rows, BLK), jnp.bfloat16),
+            pltpu.SMEM(src_ids.shape, jnp.int32),
+            pltpu.SemaphoreType.DMA,
+        ],
+        input_output_aliases={0: 0},
+        compiler_params=pltpu.CompilerParams(vmem_limit_bytes=16 << 20),
+        name="fold",
+    )(contribs, weights, trig, edge, mirror, in_hbm(src_ids))
 
 
 def remap_kernel(recv, eof_ref, out_ref, pcs_ref, eof, mixed, acc, ids_vmem, ids_smem, sem):
@@ -184,19 +252,19 @@
     cap = src_block.shape[3]
     slots = tgt_count * cap
     blocks = eofs.shape[2] // BLK
-    edge = src_vel[:, :, cells - BLK :][:, :, ::-1]
+    edge = src_vel[:, :, cells - BLK :]
     top = (src_count - 1) * tgt_count
     mirror = lax.ppermute(
-        edge, ("src", "tgt"), [(top + t, top + tgt_count - 1 - t) for t in range(tgt_count)]
+        edge[:, :, ::-1], ("src", "tgt"), [(top + t, top + tgt_count - 1 - t) for t in range(tgt_count)]
     )
     src_ids = jnp.swapaxes(src_block, 2, 3).reshape(cap, tgt_count)
     tgt_ids = jnp.swapaxes(tgt_block, 2, 3).reshape(cap, tgt_count)
     counts = send_count.reshape(tgt_count)
     weights = intersection.reshape(slots, BLK, BLK)
-    contribs = contributions(
-        src_ids, tgt_ids, counts, src_vel, angle, mirror, weights, tgt_count
+    contribs, weights, trig = contributions(
+        src_ids, tgt_ids, counts, src_vel, angle, weights, tgt_count
     )
-    contribs, eofs = lax.optimization_barrier((contribs, eofs))
+    contribs = fold(contribs, weights, trig, edge, mirror, src_ids)
     received = lax.all_to_all(contribs, "tgt", split_axis=0, concat_axis=0, tiled=True)
     remapped, partial = remap(received, eofs, rows)
     column = jnp.sum(lax.all_to_all(partial, "tgt", 0, 0, tiled=True), axis=0)

time: 83.5 us -> 81.7 us (0.978)
  Pallas kernels: 9.83 us -> 8.7 us
    pallas_call x1 -> x2, Pallas kernels: 4.77 us -> 3.66 us  [the longest x1 3.64 us: contributions(): pl.pallas_call(contribution_kernel, out_shape=(jax.ShapeDtypeStruct((peer...]
  transfers between devices with their start and end apart: 1 -> 1, of which waited for: 0 -> 0; matrix products, arithmetic and copies ran while one was open for 0% -> 0% of each run, Pallas kernels for 0% -> 4%
where the time goes in v4:
time: 81.7 us; the launch traced here: 81.4 us
  blocking collectives  69.8 us (85%)
  Pallas kernels  8.7 us (11%)
  local copies, waits for them, and re-layouts  0.93 us (1%)
    all_to_all x1, blocking collectives, per_device(): lax.all_to_all(contribs, 'tgt', split_axis=0, concat_axis=0, tiled=True)  47.7 us
    all_to_all x1, blocking collectives, per_device(): total = jnp.sum(lax.all_to_all(everyone, 'src', 0, 0, tiled=True), axis=0)  12.4 us
    all_to_all x1, blocking collectives, per_device(): column = jnp.sum(lax.all_to_all(partial, 'tgt', 0, 0, tiled=True), axis=0)  9.68 us
    pallas_call x1, Pallas kernels, remap(): pl.pallas_call(remap_kernel, out_shape=(jax.ShapeDtypeStruct((components,...  5.04 us
    pallas_call x1, Pallas kernels, contributions(): pl.pallas_call(contribution_kernel, out_shape=(jax.ShapeDtypeStruct((peer...  3.64 us
  transfers between devices with their start and end apart: 1, of which 0 were waited for; matrix products, arithmetic and copies ran while one was open for 0% of the time, Pallas kernels for 4%

profile of v4, /device:TPU:1, one launch (start us, length us, event | category | flops | bytes accessed | tf_op | source)
XLA Modules:
  0.0 81.4 jit_solution(5819455140317025224)
XLA Ops:
  0.6 0.7 slice.9.edge
  1.4 0.1 rev.3
  1.5 0.7 collective-permute-start
  2.1 0.0 slice-start
  2.1 3.6 %contributions.1 = (bf16[16,776,128]{2,1,0:T(8,128)(2,1)S(1)}, bf16[128,128,128]{2,1,0:T(8,128)(2,1)S(1)}, f32[2,32,128]{2,1,0:T(8,128)S(1)}) custom-call(s32[8,16]{1,0:T(8,128)} %bitcast.14, s32[8,16]{1,0:T(8,128)} %bitcast.17, s32[16]{0:T(128)} %bitcast.18, bf16[2,48,4096]{2,1,0:T(8,128)(2,1)} %vel_hbm.1, f32[32,128]{1,0:T(8,128)} %bitcast.16, ...), custom_call_target="tpu_custom_call" | custom-call | tf_op jit(solution)/shard_map/contributions/pallas_call | solution.py:99
  5.8 0.0 collective-permute-done.mirror
  5.8 0.0 slice-start.1
  5.8 47.7 %all_to_all.15.recv = bf16[16,776,128]{2,1,0:T(8,128)(2,1)S(1)} all-to-all(bf16[16,776,128]{2,1,0:T(8,128)(2,1)S(1)} %fold.1), channel_id=1, replica_groups=mesh['src'=8,'tgt'=16] {'tgt'}, dimensions={0} | all-to-all | bytes 6356992 | tf_op jit(solution)/shard_map/all_to_all | solution.py:268
  53.6 0.0 slice-done
  53.6 0.0 slice-done.1
  53.6 5.0 %remap.1 = (bf16[2,48,4096]{2,1,0:T(8,128)(2,1)}, f32[16,16,128]{2,1,0:T(8,128)S(1)}) custom-call(bf16[16,776,128]{2,1,0:T(8,128)(2,1)S(1)} %all_to_all.15.recv, bf16[512,2,4096]{2,1,0:T(2,128)(2,1)S(1)} %bitcast.12), custom_call_target="tpu_custom_call" | custom-call | tf_op jit(solution)/shard_map/remap/pallas_call | solution.py:227
  58.6 9.7 %all_to_all.16 = f32[16,16,128]{2,1,0:T(8,128)S(1)} all-to-all(f32[16,16,128]{2,1,0:T(8,128)S(1)} %get-tuple-element.11), channel_id=1, replica_groups=mesh['src'=8,'tgt'=16] {'tgt'}, dimensions={0} | all-to-all | bytes 262144 | tf_op jit(solution)/shard_map/all_to_all | solution.py:270
  68.3 12.4 %all_to_all.17 = f32[8,16,128]{2,1,0:T(8,128)S(1)} all-to-all(f32[8,16,128]{2,1,0:T(8,128)S(1)} %broadcast_in_dim.2), channel_id=1, replica_groups=mesh['src'=8,'tgt'=16] {'src'}, dimensions={0} | all-to-all | bytes 131072 | tf_op jit(solution)/shard_map/all_to_all | solution.py:272
  80.7 0.1 fusion
  80.8 0.6 maximum_bitcast_fusion
  (5 shorter events, 0.1 us)
Async XLA Ops:
  1.5 4.3 %collective-permute-start = (bf16[2,48,128]{2,1,0:T(8,128)(2,1)S(1)}, bf16[2,48,128]{2,1,0:T(8,128)(2,1)S(1)}, u32[]{:S(2)}, u32[]{:S(2)}) collective-permute-start(bf16[2,48,128]{2,1,0:T(8,128)(2,1)S(1)} %rev.3), channel_id=1, source_target_pairs={{112,127},{113,126},{114,125},{115,124},{116,123},{117,122},{118,1... | collective-permute-start | bytes 73736 | tf_op jit(solution)/shard_map/ppermute | solution.py:257
  2.1 51.4 %slice-start = ((s8[8388608]{0:T(1024)(128)(4,1)}), s8[4194304]{0:T(1024)(128)(4,1)S(1)}, s32[]{:S(2)}) async-start(s8[8388608]{0:T(1024)(128)(4,1)} %bitcast.11), calls=%async_computation.3 | async-start | bytes 8388608
  5.8 47.8 %slice-start.1 = ((s8[8388608]{0:T(1024)(128)(4,1)}), s8[4194304]{0:T(1024)(128)(4,1)S(1)}, s32[]{:S(2)}) async-start(s8[8388608]{0:T(1024)(128)(4,1)} %bitcast.11), calls=%async_computation.4 | async-start | bytes 8388608

commit v5 on v4

--- a/solution.py
+++ b/solution.py
@@ -245,6 +245,10 @@
     )(received, eofs)
 
 
+def from_row(x, to):
+    return lax.ppermute(x, "src", [(row, to(row)) for row in range(lax.axis_size("src"))])
+
+
 def per_device(src_vel, angle, src_block, tgt_block, send_count, intersection, eofs):
     components, rows, cells = src_vel.shape
     src_count = lax.axis_size("src")
@@ -268,8 +272,11 @@
     received = lax.all_to_all(contribs, "tgt", split_axis=0, concat_axis=0, tiled=True)
     remapped, partial = remap(received, eofs, rows)
     column = jnp.sum(lax.all_to_all(partial, "tgt", 0, 0, tiled=True), axis=0)
-    everyone = jnp.broadcast_to(column[None], (src_count, *column.shape))
-    total = jnp.sum(lax.all_to_all(everyone, "src", 0, 0, tiled=True), axis=0)
+    pair = column + from_row(column, lambda row: row ^ 1)
+    one, two, three = (
+        from_row(pair, lambda row, k=k: (row + 2 * k) % src_count) for k in range(1, src_count // 2)
+    )
+    total = (pair + two) + (one + three)
     pcs = jnp.concatenate([total[:, :rows], total[:, BLK // 2 : BLK // 2 + rows]], axis=0).T
     return remapped, pcs
 

time: 81.7 us -> 80.3 us (0.983)
  blocking collectives: 69.8 us -> 57.4 us
  starting transfers between devices: 0.65 us -> 8.33 us
  waiting for transfers between devices: 0.01 us -> 2.99 us
    all_to_all x1 -> x0, blocking collectives: 12.4 us -> none  [per_device(): total = jnp.sum(lax.all_to_all(everyone, 'src', 0, 0, tiled=True), axis=0)]
    ppermute x0 -> x4, starting transfers between devices: none -> 7.68 us  [from_row(): lax.ppermute(x, 'src', [(row, to(row)) for row in range(lax.axis_size('sr...]
    ppermute x0 -> x4, waiting for transfers between devices: none -> 2.98 us  [from_row(): lax.ppermute(x, 'src', [(row, to(row)) for row in range(lax.axis_size('sr...]
  transfers between devices with their start and end apart: 1 -> 5, of which waited for: 0 -> 3; matrix products, arithmetic and copies ran while one was open for 0% -> 0% of each run, Pallas kernels for 4% -> 5%
where the time goes in v5:
time: 80.3 us; the launch traced here: 79.7 us
  blocking collectives  57.4 us (71%)
  Pallas kernels  8.76 us (11%)
  starting transfers between devices  8.33 us (10%)
  waiting for transfers between devices  2.99 us (4%)
  local copies, waits for them, and re-layouts  0.93 us (1%)
    all_to_all x1, blocking collectives, per_device(): lax.all_to_all(contribs, 'tgt', split_axis=0, concat_axis=0, tiled=True)  47.7 us
    all_to_all x1, blocking collectives, per_device(): column = jnp.sum(lax.all_to_all(partial, 'tgt', 0, 0, tiled=True), axis=0)  9.65 us
    ppermute x4, starting transfers between devices, from_row(): lax.ppermute(x, 'src', [(row, to(row)) for row in range(lax.axis_size('sr...  7.68 us
    pallas_call x1, Pallas kernels, remap(): pl.pallas_call(remap_kernel, out_shape=(jax.ShapeDtypeStruct((components,...  5.1 us
    pallas_call x1, Pallas kernels, contributions(): pl.pallas_call(contribution_kernel, out_shape=(jax.ShapeDtypeStruct((peer...  3.63 us
    ppermute x4, waiting for transfers between devices, from_row(): lax.ppermute(x, 'src', [(row, to(row)) for row in range(lax.axis_size('sr...  2.98 us
  transfers between devices with their start and end apart: 5, of which 3 were waited for; matrix products, arithmetic and copies ran while one was open for 0% of the time, Pallas kernels for 5%

profile of v5, /device:TPU:1, one launch (start us, length us, event | category | flops | bytes accessed | tf_op | source)
XLA Modules:
  0.0 79.7 jit_solution(1518991265244561628)
XLA Ops:
  0.6 0.7 slice.9.edge
  1.4 0.1 rev.3
  1.5 0.7 collective-permute-start
  2.1 0.0 slice-start
  2.1 3.6 %contributions.1 = (bf16[16,776,128]{2,1,0:T(8,128)(2,1)S(1)}, bf16[128,128,128]{2,1,0:T(8,128)(2,1)S(1)}, f32[2,32,128]{2,1,0:T(8,128)S(1)}) custom-call(s32[8,16]{1,0:T(8,128)} %bitcast.14, s32[8,16]{1,0:T(8,128)} %bitcast.17, s32[16]{0:T(128)} %bitcast.18, bf16[2,48,4096]{2,1,0:T(8,128)(2,1)} %vel_hbm.1, f32[32,128]{1,0:T(8,128)} %bitcast.16, ...), custom_call_target="tpu_custom_call" | custom-call | tf_op jit(solution)/shard_map/contributions/pallas_call | solution.py:99
  5.8 0.0 collective-permute-done.mirror
  5.8 0.0 slice-start.1
  5.8 47.7 %all_to_all.10.recv = bf16[16,776,128]{2,1,0:T(8,128)(2,1)S(1)} all-to-all(bf16[16,776,128]{2,1,0:T(8,128)(2,1)S(1)} %fold.1), channel_id=1, replica_groups=mesh['src'=8,'tgt'=16] {'tgt'}, dimensions={0} | all-to-all | bytes 6356992 | tf_op jit(solution)/shard_map/all_to_all | solution.py:272
  53.6 0.0 slice-done
  53.6 0.0 slice-done.1
  53.6 5.1 %remap.1 = (bf16[2,48,4096]{2,1,0:T(8,128)(2,1)}, f32[16,16,128]{2,1,0:T(8,128)S(1)}) custom-call(bf16[16,776,128]{2,1,0:T(8,128)(2,1)S(1)} %all_to_all.10.recv, bf16[512,2,4096]{2,1,0:T(2,128)(2,1)S(1)} %bitcast.12), custom_call_target="tpu_custom_call" | custom-call | tf_op jit(solution)/shard_map/remap/pallas_call | solution.py:227
  58.7 9.7 %all_to_all.11 = f32[16,16,128]{2,1,0:T(8,128)S(1)} all-to-all(f32[16,16,128]{2,1,0:T(8,128)S(1)} %get-tuple-element.11), channel_id=1, replica_groups=mesh['src'=8,'tgt'=16] {'tgt'}, dimensions={0} | all-to-all | bytes 262144 | tf_op jit(solution)/shard_map/all_to_all | solution.py:274
  68.3 3.3 %collective-permute-start.1 = (f32[16,128]{1,0:T(8,128)S(1)}, f32[16,128]{1,0:T(8,128)S(1)}, u32[]{:S(2)}, u32[]{:S(2)}) collective-permute-start(f32[16,128]{1,0:T(8,128)S(1)} %reduce_sum.9), channel_id=1, source_target_pairs={{0,16},{16,0},{32,48},{48,32},{64,80},{80,64},{96,112},{112,96},{1... | collective-permute-start | bytes 24584 | tf_op jit(solution)/shard_map/ppermute | solution.py:249
  71.7 0.8 %collective-permute-done.1 = f32[16,128]{1,0:T(8,128)S(1)} collective-permute-done((f32[16,128]{1,0:T(8,128)S(1)}, f32[16,128]{1,0:T(8,128)S(1)}, u32[]{:S(2)}, u32[]{:S(2)}) %collective-permute-start.1) | collective-permute-done | bytes 8224 | tf_op jit(solution)/shard_map/ppermute | solution.py:249
  72.5 2.4 %collective-permute-start.4 = (f32[16,128]{1,0:T(8,128)S(1)}, f32[16,128]{1,0:T(8,128)S(1)}, u32[]{:S(2)}, u32[]{:S(2)}) collective-permute-start(f32[16,128]{1,0:T(8,128)S(1)} %add.12), channel_id=1, source_target_pairs={{0,96},{16,112},{32,0},{48,16},{64,32},{80,48},{96,64},{112,80},{1... | collective-permute-start | bytes 24584 | tf_op jit(solution)/shard_map/ppermute | solution.py:249
  74.9 0.0 collective-permute-start.3
  75.0 1.9 %collective-permute-start.2 = (f32[16,128]{1,0:T(8,128)S(1)}, f32[16,128]{1,0:T(8,128)S(1)}, u32[]{:S(2)}, u32[]{:S(2)}) collective-permute-start(f32[16,128]{1,0:T(8,128)S(1)} %add.12), channel_id=1, source_target_pairs={{0,64},{16,80},{32,96},{48,112},{64,0},{80,16},{96,32},{112,48},{1... | collective-permute-start | bytes 24584 | tf_op jit(solution)/shard_map/ppermute | solution.py:249
  76.9 0.0 collective-permute-done.4
  76.9 1.8 %collective-permute-done.3 = f32[16,128]{1,0:T(8,128)S(1)} collective-permute-done((f32[16,128]{1,0:T(8,128)S(1)}, f32[16,128]{1,0:T(8,128)S(1)}, u32[]{:S(2)}, u32[]{:S(2)}) %collective-permute-start.3) | collective-permute-done | bytes 8224 | tf_op jit(solution)/shard_map/ppermute | solution.py:249
  78.7 0.4 collective-permute-done.2
  79.0 0.1 fusion
  79.1 0.6 maximum_bitcast_fusion
  (5 shorter events, 0.1 us)
Async XLA Ops:
  1.5 4.3 %collective-permute-start = (bf16[2,48,128]{2,1,0:T(8,128)(2,1)S(1)}, bf16[2,48,128]{2,1,0:T(8,128)(2,1)S(1)}, u32[]{:S(2)}, u32[]{:S(2)}) collective-permute-start(bf16[2,48,128]{2,1,0:T(8,128)(2,1)S(1)} %rev.3), channel_id=1, source_target_pairs={{112,127},{113,126},{114,125},{115,124},{116,123},{117,122},{118,1... | collective-permute-start | bytes 73736 | tf_op jit(solution)/shard_map/ppermute | solution.py:261
  2.1 51.4 %slice-start = ((s8[8388608]{0:T(1024)(128)(4,1)}), s8[4194304]{0:T(1024)(128)(4,1)S(1)}, s32[]{:S(2)}) async-start(s8[8388608]{0:T(1024)(128)(4,1)} %bitcast.11), calls=%async_computation.2 | async-start | bytes 8388608
  5.8 47.8 %slice-start.1 = ((s8[8388608]{0:T(1024)(128)(4,1)}), s8[4194304]{0:T(1024)(128)(4,1)S(1)}, s32[]{:S(2)}) async-start(s8[8388608]{0:T(1024)(128)(4,1)} %bitcast.11), calls=%async_computation.3 | async-start | bytes 8388608
  68.3 4.2 %collective-permute-start.1 = (f32[16,128]{1,0:T(8,128)S(1)}, f32[16,128]{1,0:T(8,128)S(1)}, u32[]{:S(2)}, u32[]{:S(2)}) collective-permute-start(f32[16,128]{1,0:T(8,128)S(1)} %reduce_sum.9), channel_id=1, source_target_pairs={{0,16},{16,0},{32,48},{48,32},{64,80},{80,64},{96,112},{112,96},{1... | collective-permute-start | bytes 24584 | tf_op jit(solution)/shard_map/ppermute | solution.py:249
  72.5 4.4 %collective-permute-start.4 = (f32[16,128]{1,0:T(8,128)S(1)}, f32[16,128]{1,0:T(8,128)S(1)}, u32[]{:S(2)}, u32[]{:S(2)}) collective-permute-start(f32[16,128]{1,0:T(8,128)S(1)} %add.12), channel_id=1, source_target_pairs={{0,96},{16,112},{32,0},{48,16},{64,32},{80,48},{96,64},{112,80},{1... | collective-permute-start | bytes 24584 | tf_op jit(solution)/shard_map/ppermute | solution.py:249
  74.9 3.7 %collective-permute-start.3 = (f32[16,128]{1,0:T(8,128)S(1)}, f32[16,128]{1,0:T(8,128)S(1)}, u32[]{:S(2)}, u32[]{:S(2)}) collective-permute-start(f32[16,128]{1,0:T(8,128)S(1)} %add.12), channel_id=1, source_target_pairs={{0,32},{16,48},{32,64},{48,80},{64,96},{80,112},{96,0},{112,16},{1... | collective-permute-start | bytes 24584 | tf_op jit(solution)/shard_map/ppermute | solution.py:249
  75.0 4.1 %collective-permute-start.2 = (f32[16,128]{1,0:T(8,128)S(1)}, f32[16,128]{1,0:T(8,128)S(1)}, u32[]{:S(2)}, u32[]{:S(2)}) collective-permute-start(f32[16,128]{1,0:T(8,128)S(1)} %add.12), channel_id=1, source_target_pairs={{0,64},{16,80},{32,96},{48,112},{64,0},{80,16},{96,32},{112,48},{1... | collective-permute-start | bytes 24584 | tf_op jit(solution)/shard_map/ppermute | solution.py:249

commit v6 on v5

--- a/solution.py
+++ b/solution.py
@@ -8,7 +8,7 @@
 BLK = 128
 ID_ROWS = 8
 W_CHUNK = 64
-EOF_PARTS = 2
+EOF_PARTS = 1
 
 
 def in_hbm(x):
@@ -135,8 +135,13 @@
     def _():
         copy = pltpu.make_async_copy(ids_hbm, ids, sem)
         copy.start()
-        x = 0.5 * (edge[0].astype(jnp.float32) - mirror[0].astype(jnp.float32))
-        y = 0.5 * (edge[1].astype(jnp.float32) - mirror[1].astype(jnp.float32))
+        lane = lax.broadcasted_iota(jnp.int32, (BLK, BLK), 0)
+        flip = (lane + lax.broadcasted_iota(jnp.int32, (BLK, BLK), 1) == BLK - 1).astype(jnp.float32)
+        flip = flip.astype(jnp.bfloat16)
+        x, y = (
+            0.5 * (edge[c].astype(jnp.float32) - jnp.dot(mirror[c], flip, preferred_element_type=jnp.float32))
+            for c in range(2)
+        )
         c = trig[0, blocks - 1 : blocks, :]
         s = trig[1, blocks - 1 : blocks, :]
         block[:rows, :] = (c * x - s * y).astype(jnp.bfloat16)
@@ -194,7 +199,7 @@
             acc[pl.ds(start, height), :] += part
         return carry
 
-    lax.fori_loop(0, peers, sender, 0)
+    lax.fori_loop(0, peers, sender, 0, unroll=2)
     for b in range(blocks):
         total = acc[b * height : (b + 1) * height, :].astype(jnp.bfloat16)
         for c in range(components):
@@ -259,7 +264,7 @@
     edge = src_vel[:, :, cells - BLK :]
     top = (src_count - 1) * tgt_count
     mirror = lax.ppermute(
-        edge[:, :, ::-1], ("src", "tgt"), [(top + t, top + tgt_count - 1 - t) for t in range(tgt_count)]
+        edge, ("src", "tgt"), [(top + t, top + tgt_count - 1 - t) for t in range(tgt_count)]
     )
     src_ids = jnp.swapaxes(src_block, 2, 3).reshape(cap, tgt_count)
     tgt_ids = jnp.swapaxes(tgt_block, 2, 3).reshape(cap, tgt_count)

time: 80.3 us -> 80.1 us (level)
  no operation moved by 1% of the time
where the time goes in v6:
time: 80.1 us; the launch traced here: 79.6 us
  blocking collectives  57.4 us (72%)
  Pallas kernels  8.64 us (11%)
  starting transfers between devices  8.31 us (10%)
  waiting for transfers between devices  3.04 us (4%)
  local copies, waits for them, and re-layouts  0.83 us (1%)
    all_to_all x1, blocking collectives, per_device(): lax.all_to_all(contribs, 'tgt', split_axis=0, concat_axis=0, tiled=True)  47.7 us
    all_to_all x1, blocking collectives, per_device(): column = jnp.sum(lax.all_to_all(partial, 'tgt', 0, 0, tiled=True), axis=0)  9.73 us
    ppermute x4, starting transfers between devices, from_row(): lax.ppermute(x, 'src', [(row, to(row)) for row in range(lax.axis_size('sr...  7.66 us
    pallas_call x1, Pallas kernels, remap(): pl.pallas_call(remap_kernel, out_shape=(jax.ShapeDtypeStruct((components,...  4.99 us
    pallas_call x1, Pallas kernels, contributions(): pl.pallas_call(contribution_kernel, out_shape=(jax.ShapeDtypeStruct((peer...  3.63 us
    ppermute x4, waiting for transfers between devices, from_row(): lax.ppermute(x, 'src', [(row, to(row)) for row in range(lax.axis_size('sr...  3.03 us
  transfers between devices with their start and end apart: 5, of which 3 were waited for; matrix products, arithmetic and copies ran while one was open for 0% of the time, Pallas kernels for 5%

profile of v6, /device:TPU:1, one launch (start us, length us, event | category | flops | bytes accessed | tf_op | source)
XLA Modules:
  0.0 79.6 jit_solution(6751112588195126443)
XLA Ops:
  0.6 0.7 slice.9.edge
  1.4 0.7 collective-permute-start
  2.0 0.0 slice-start
  2.0 3.6 %contributions.1 = (bf16[16,776,128]{2,1,0:T(8,128)(2,1)S(1)}, bf16[128,128,128]{2,1,0:T(8,128)(2,1)S(1)}, f32[2,32,128]{2,1,0:T(8,128)S(1)}) custom-call(s32[8,16]{1,0:T(8,128)} %bitcast.14, s32[8,16]{1,0:T(8,128)} %bitcast.17, s32[16]{0:T(128)} %bitcast.18, bf16[2,48,4096]{2,1,0:T(8,128)(2,1)} %vel_hbm.1, f32[32,128]{1,0:T(8,128)} %bitcast.16, ...), custom_call_target="tpu_custom_call" | custom-call | tf_op jit(solution)/shard_map/contributions/pallas_call | solution.py:99
  5.7 0.0 collective-permute-done.mirror
  5.7 0.0 slice-start.1
  5.7 47.7 %all_to_all.10.recv = bf16[16,776,128]{2,1,0:T(8,128)(2,1)S(1)} all-to-all(bf16[16,776,128]{2,1,0:T(8,128)(2,1)S(1)} %fold.1), channel_id=1, replica_groups=mesh['src'=8,'tgt'=16] {'tgt'}, dimensions={0} | all-to-all | bytes 6356992 | tf_op jit(solution)/shard_map/all_to_all | solution.py:277
  53.5 0.0 slice-done
  53.5 0.0 slice-done.1
  53.5 5.0 %remap.1 = (bf16[2,48,4096]{2,1,0:T(8,128)(2,1)}, f32[16,16,128]{2,1,0:T(8,128)S(1)}) custom-call(bf16[16,776,128]{2,1,0:T(8,128)(2,1)S(1)} %all_to_all.10.recv, bf16[512,2,4096]{2,1,0:T(2,128)(2,1)S(1)} %bitcast.12), custom_call_target="tpu_custom_call" | custom-call | tf_op jit(solution)/shard_map/remap/pallas_call | solution.py:232
  58.5 9.7 %all_to_all.11 = f32[16,16,128]{2,1,0:T(8,128)S(1)} all-to-all(f32[16,16,128]{2,1,0:T(8,128)S(1)} %get-tuple-element.11), channel_id=1, replica_groups=mesh['src'=8,'tgt'=16] {'tgt'}, dimensions={0} | all-to-all | bytes 262144 | tf_op jit(solution)/shard_map/all_to_all | solution.py:279
  68.2 3.3 %collective-permute-start.1 = (f32[16,128]{1,0:T(8,128)S(1)}, f32[16,128]{1,0:T(8,128)S(1)}, u32[]{:S(2)}, u32[]{:S(2)}) collective-permute-start(f32[16,128]{1,0:T(8,128)S(1)} %reduce_sum.9), channel_id=1, source_target_pairs={{0,16},{16,0},{32,48},{48,32},{64,80},{80,64},{96,112},{112,96},{1... | collective-permute-start | bytes 24584 | tf_op jit(solution)/shard_map/ppermute | solution.py:254
  71.5 0.8 %collective-permute-done.1 = f32[16,128]{1,0:T(8,128)S(1)} collective-permute-done((f32[16,128]{1,0:T(8,128)S(1)}, f32[16,128]{1,0:T(8,128)S(1)}, u32[]{:S(2)}, u32[]{:S(2)}) %collective-permute-start.1) | collective-permute-done | bytes 8224 | tf_op jit(solution)/shard_map/ppermute | solution.py:254
  72.4 2.5 %collective-permute-start.4 = (f32[16,128]{1,0:T(8,128)S(1)}, f32[16,128]{1,0:T(8,128)S(1)}, u32[]{:S(2)}, u32[]{:S(2)}) collective-permute-start(f32[16,128]{1,0:T(8,128)S(1)} %add.12), channel_id=1, source_target_pairs={{0,96},{16,112},{32,0},{48,16},{64,32},{80,48},{96,64},{112,80},{1... | collective-permute-start | bytes 24584 | tf_op jit(solution)/shard_map/ppermute | solution.py:254
  74.9 0.0 collective-permute-start.3
  74.9 1.8 %collective-permute-start.2 = (f32[16,128]{1,0:T(8,128)S(1)}, f32[16,128]{1,0:T(8,128)S(1)}, u32[]{:S(2)}, u32[]{:S(2)}) collective-permute-start(f32[16,128]{1,0:T(8,128)S(1)} %add.12), channel_id=1, source_target_pairs={{0,64},{16,80},{32,96},{48,112},{64,0},{80,16},{96,32},{112,48},{1... | collective-permute-start | bytes 24584 | tf_op jit(solution)/shard_map/ppermute | solution.py:254
  76.7 0.0 collective-permute-done.4
  76.7 1.9 %collective-permute-done.3 = f32[16,128]{1,0:T(8,128)S(1)} collective-permute-done((f32[16,128]{1,0:T(8,128)S(1)}, f32[16,128]{1,0:T(8,128)S(1)}, u32[]{:S(2)}, u32[]{:S(2)}) %collective-permute-start.3) | collective-permute-done | bytes 8224 | tf_op jit(solution)/shard_map/ppermute | solution.py:254
  78.6 0.3 collective-permute-done.2
  78.9 0.1 fusion
  79.0 0.6 maximum_bitcast_fusion
  (5 shorter events, 0.1 us)
Async XLA Ops:
  1.4 4.3 %collective-permute-start = (bf16[2,48,128]{2,1,0:T(8,128)(2,1)S(1)}, bf16[2,48,128]{2,1,0:T(8,128)(2,1)S(1)}, u32[]{:S(2)}, u32[]{:S(2)}) collective-permute-start(bf16[2,48,128]{2,1,0:T(8,128)(2,1)S(1)} %slice.9.edge), channel_id=1, source_target_pairs={{112,127},{113,126},{114,125},{115,124},{116,123},{117,122},{118,1... | collective-permute-start | bytes 73736 | tf_op jit(solution)/shard_map/ppermute | solution.py:266
  2.0 51.4 %slice-start = ((s8[8388608]{0:T(1024)(128)(4,1)}), s8[4194304]{0:T(1024)(128)(4,1)S(1)}, s32[]{:S(2)}) async-start(s8[8388608]{0:T(1024)(128)(4,1)} %bitcast.11), calls=%async_computation.2 | async-start | bytes 8388608
  5.7 47.8 %slice-start.1 = ((s8[8388608]{0:T(1024)(128)(4,1)}), s8[4194304]{0:T(1024)(128)(4,1)S(1)}, s32[]{:S(2)}) async-start(s8[8388608]{0:T(1024)(128)(4,1)} %bitcast.11), calls=%async_computation.3 | async-start | bytes 8388608
  68.2 4.2 %collective-permute-start.1 = (f32[16,128]{1,0:T(8,128)S(1)}, f32[16,128]{1,0:T(8,128)S(1)}, u32[]{:S(2)}, u32[]{:S(2)}) collective-permute-start(f32[16,128]{1,0:T(8,128)S(1)} %reduce_sum.9), channel_id=1, source_target_pairs={{0,16},{16,0},{32,48},{48,32},{64,80},{80,64},{96,112},{112,96},{1... | collective-permute-start | bytes 24584 | tf_op jit(solution)/shard_map/ppermute | solution.py:254
  72.4 4.3 %collective-permute-start.4 = (f32[16,128]{1,0:T(8,128)S(1)}, f32[16,128]{1,0:T(8,128)S(1)}, u32[]{:S(2)}, u32[]{:S(2)}) collective-permute-start(f32[16,128]{1,0:T(8,128)S(1)} %add.12), channel_id=1, source_target_pairs={{0,96},{16,112},{32,0},{48,16},{64,32},{80,48},{96,64},{112,80},{1... | collective-permute-start | bytes 24584 | tf_op jit(solution)/shard_map/ppermute | solution.py:254
  74.9 3.7 %collective-permute-start.3 = (f32[16,128]{1,0:T(8,128)S(1)}, f32[16,128]{1,0:T(8,128)S(1)}, u32[]{:S(2)}, u32[]{:S(2)}) collective-permute-start(f32[16,128]{1,0:T(8,128)S(1)} %add.12), channel_id=1, source_target_pairs={{0,32},{16,48},{32,64},{48,80},{64,96},{80,112},{96,0},{112,16},{1... | collective-permute-start | bytes 24584 | tf_op jit(solution)/shard_map/ppermute | solution.py:254
  74.9 4.1 %collective-permute-start.2 = (f32[16,128]{1,0:T(8,128)S(1)}, f32[16,128]{1,0:T(8,128)S(1)}, u32[]{:S(2)}, u32[]{:S(2)}) collective-permute-start(f32[16,128]{1,0:T(8,128)S(1)} %add.12), channel_id=1, source_target_pairs={{0,64},{16,80},{32,96},{48,112},{64,0},{80,16},{96,32},{112,48},{1... | collective-permute-start | bytes 24584 | tf_op jit(solution)/shard_map/ppermute | solution.py:254

commit v7 on v6

--- a/solution.py
+++ b/solution.py
@@ -199,7 +199,7 @@
             acc[pl.ds(start, height), :] += part
         return carry
 
-    lax.fori_loop(0, peers, sender, 0, unroll=2)
+    lax.fori_loop(0, peers, sender, 0, unroll=True)
     for b in range(blocks):
         total = acc[b * height : (b + 1) * height, :].astype(jnp.bfloat16)
         for c in range(components):

time: 80.1 us -> 80.1 us (level)
  no operation moved by 1% of the time
where the time goes in v7:
time: 80.1 us; the launch traced here: 79.6 us
  blocking collectives  57.3 us (72%)
  Pallas kernels  8.66 us (11%)
  starting transfers between devices  8.39 us (10%)
  waiting for transfers between devices  3.07 us (4%)
  local copies, waits for them, and re-layouts  0.83 us (1%)
    all_to_all x1, blocking collectives, per_device(): lax.all_to_all(contribs, 'tgt', split_axis=0, concat_axis=0, tiled=True)  47.7 us
    all_to_all x1, blocking collectives, per_device(): column = jnp.sum(lax.all_to_all(partial, 'tgt', 0, 0, tiled=True), axis=0)  9.59 us
    ppermute x4, starting transfers between devices, from_row(): lax.ppermute(x, 'src', [(row, to(row)) for row in range(lax.axis_size('sr...  7.74 us
    pallas_call x1, Pallas kernels, remap(): pl.pallas_call(remap_kernel, out_shape=(jax.ShapeDtypeStruct((components,...  5 us
    pallas_call x1, Pallas kernels, contributions(): pl.pallas_call(contribution_kernel, out_shape=(jax.ShapeDtypeStruct((peer...  3.64 us
    ppermute x4, waiting for transfers between devices, from_row(): lax.ppermute(x, 'src', [(row, to(row)) for row in range(lax.axis_size('sr...  3.06 us
  transfers between devices with their start and end apart: 5, of which 3 were waited for; matrix products, arithmetic and copies ran while one was open for 0% of the time, Pallas kernels for 5%

profile of v7, /device:TPU:1, one launch (start us, length us, event | category | flops | bytes accessed | tf_op | source)
XLA Modules:
  0.0 79.6 jit_solution(5568022102165259605)
XLA Ops:
  0.6 0.7 slice.9.edge
  1.4 0.7 collective-permute-start
  2.0 0.0 slice-start
  2.0 3.6 %contributions.1 = (bf16[16,776,128]{2,1,0:T(8,128)(2,1)S(1)}, bf16[128,128,128]{2,1,0:T(8,128)(2,1)S(1)}, f32[2,32,128]{2,1,0:T(8,128)S(1)}) custom-call(s32[8,16]{1,0:T(8,128)} %bitcast.14, s32[8,16]{1,0:T(8,128)} %bitcast.17, s32[16]{0:T(128)} %bitcast.18, bf16[2,48,4096]{2,1,0:T(8,128)(2,1)} %vel_hbm.1, f32[32,128]{1,0:T(8,128)} %bitcast.16, ...), custom_call_target="tpu_custom_call" | custom-call | tf_op jit(solution)/shard_map/contributions/pallas_call | solution.py:99
  5.7 0.0 collective-permute-done.mirror
  5.7 0.0 slice-start.1
  5.7 47.7 %all_to_all.10.recv = bf16[16,776,128]{2,1,0:T(8,128)(2,1)S(1)} all-to-all(bf16[16,776,128]{2,1,0:T(8,128)(2,1)S(1)} %fold.1), channel_id=1, replica_groups=mesh['src'=8,'tgt'=16] {'tgt'}, dimensions={0} | all-to-all | bytes 6356992 | tf_op jit(solution)/shard_map/all_to_all | solution.py:277
  53.5 0.0 slice-done
  53.5 0.0 slice-done.1
  53.5 5.0 %remap.1 = (bf16[2,48,4096]{2,1,0:T(8,128)(2,1)}, f32[16,16,128]{2,1,0:T(8,128)S(1)}) custom-call(bf16[16,776,128]{2,1,0:T(8,128)(2,1)S(1)} %all_to_all.10.recv, bf16[512,2,4096]{2,1,0:T(2,128)(2,1)S(1)} %bitcast.12), custom_call_target="tpu_custom_call" | custom-call | tf_op jit(solution)/shard_map/remap/pallas_call | solution.py:232
  58.5 9.6 %all_to_all.11 = f32[16,16,128]{2,1,0:T(8,128)S(1)} all-to-all(f32[16,16,128]{2,1,0:T(8,128)S(1)} %get-tuple-element.11), channel_id=1, replica_groups=mesh['src'=8,'tgt'=16] {'tgt'}, dimensions={0} | all-to-all | bytes 262144 | tf_op jit(solution)/shard_map/all_to_all | solution.py:279
  68.1 3.3 %collective-permute-start.1 = (f32[16,128]{1,0:T(8,128)S(1)}, f32[16,128]{1,0:T(8,128)S(1)}, u32[]{:S(2)}, u32[]{:S(2)}) collective-permute-start(f32[16,128]{1,0:T(8,128)S(1)} %reduce_sum.9), channel_id=1, source_target_pairs={{0,16},{16,0},{32,48},{48,32},{64,80},{80,64},{96,112},{112,96},{1... | collective-permute-start | bytes 24584 | tf_op jit(solution)/shard_map/ppermute | solution.py:254
  71.4 0.8 %collective-permute-done.1 = f32[16,128]{1,0:T(8,128)S(1)} collective-permute-done((f32[16,128]{1,0:T(8,128)S(1)}, f32[16,128]{1,0:T(8,128)S(1)}, u32[]{:S(2)}, u32[]{:S(2)}) %collective-permute-start.1) | collective-permute-done | bytes 8224 | tf_op jit(solution)/shard_map/ppermute | solution.py:254
  72.2 2.6 %collective-permute-start.4 = (f32[16,128]{1,0:T(8,128)S(1)}, f32[16,128]{1,0:T(8,128)S(1)}, u32[]{:S(2)}, u32[]{:S(2)}) collective-permute-start(f32[16,128]{1,0:T(8,128)S(1)} %add.12), channel_id=1, source_target_pairs={{0,96},{16,112},{32,0},{48,16},{64,32},{80,48},{96,64},{112,80},{1... | collective-permute-start | bytes 24584 | tf_op jit(solution)/shard_map/ppermute | solution.py:254
  74.9 0.0 collective-permute-start.3
  74.9 1.8 %collective-permute-start.2 = (f32[16,128]{1,0:T(8,128)S(1)}, f32[16,128]{1,0:T(8,128)S(1)}, u32[]{:S(2)}, u32[]{:S(2)}) collective-permute-start(f32[16,128]{1,0:T(8,128)S(1)} %add.12), channel_id=1, source_target_pairs={{0,64},{16,80},{32,96},{48,112},{64,0},{80,16},{96,32},{112,48},{1... | collective-permute-start | bytes 24584 | tf_op jit(solution)/shard_map/ppermute | solution.py:254
  76.7 0.0 collective-permute-done.4
  76.7 1.9 %collective-permute-done.3 = f32[16,128]{1,0:T(8,128)S(1)} collective-permute-done((f32[16,128]{1,0:T(8,128)S(1)}, f32[16,128]{1,0:T(8,128)S(1)}, u32[]{:S(2)}, u32[]{:S(2)}) %collective-permute-start.3) | collective-permute-done | bytes 8224 | tf_op jit(solution)/shard_map/ppermute | solution.py:254
  78.6 0.3 collective-permute-done.2
  78.9 0.1 fusion
  79.0 0.6 maximum_bitcast_fusion
  (5 shorter events, 0.1 us)
Async XLA Ops:
  1.4 4.3 %collective-permute-start = (bf16[2,48,128]{2,1,0:T(8,128)(2,1)S(1)}, bf16[2,48,128]{2,1,0:T(8,128)(2,1)S(1)}, u32[]{:S(2)}, u32[]{:S(2)}) collective-permute-start(bf16[2,48,128]{2,1,0:T(8,128)(2,1)S(1)} %slice.9.edge), channel_id=1, source_target_pairs={{112,127},{113,126},{114,125},{115,124},{116,123},{117,122},{118,1... | collective-permute-start | bytes 73736 | tf_op jit(solution)/shard_map/ppermute | solution.py:266
  2.0 51.4 %slice-start = ((s8[8388608]{0:T(1024)(128)(4,1)}), s8[4194304]{0:T(1024)(128)(4,1)S(1)}, s32[]{:S(2)}) async-start(s8[8388608]{0:T(1024)(128)(4,1)} %bitcast.11), calls=%async_computation.2 | async-start | bytes 8388608
  5.7 47.8 %slice-start.1 = ((s8[8388608]{0:T(1024)(128)(4,1)}), s8[4194304]{0:T(1024)(128)(4,1)S(1)}, s32[]{:S(2)}) async-start(s8[8388608]{0:T(1024)(128)(4,1)} %bitcast.11), calls=%async_computation.3 | async-start | bytes 8388608
  68.1 4.2 %collective-permute-start.1 = (f32[16,128]{1,0:T(8,128)S(1)}, f32[16,128]{1,0:T(8,128)S(1)}, u32[]{:S(2)}, u32[]{:S(2)}) collective-permute-start(f32[16,128]{1,0:T(8,128)S(1)} %reduce_sum.9), channel_id=1, source_target_pairs={{0,16},{16,0},{32,48},{48,32},{64,80},{80,64},{96,112},{112,96},{1... | collective-permute-start | bytes 24584 | tf_op jit(solution)/shard_map/ppermute | solution.py:254
  72.2 4.4 %collective-permute-start.4 = (f32[16,128]{1,0:T(8,128)S(1)}, f32[16,128]{1,0:T(8,128)S(1)}, u32[]{:S(2)}, u32[]{:S(2)}) collective-permute-start(f32[16,128]{1,0:T(8,128)S(1)} %add.12), channel_id=1, source_target_pairs={{0,96},{16,112},{32,0},{48,16},{64,32},{80,48},{96,64},{112,80},{1... | collective-permute-start | bytes 24584 | tf_op jit(solution)/shard_map/ppermute | solution.py:254
  74.9 3.7 %collective-permute-start.3 = (f32[16,128]{1,0:T(8,128)S(1)}, f32[16,128]{1,0:T(8,128)S(1)}, u32[]{:S(2)}, u32[]{:S(2)}) collective-permute-start(f32[16,128]{1,0:T(8,128)S(1)} %add.12), channel_id=1, source_target_pairs={{0,32},{16,48},{32,64},{48,80},{64,96},{80,112},{96,0},{112,16},{1... | collective-permute-start | bytes 24584 | tf_op jit(solution)/shard_map/ppermute | solution.py:254
  74.9 4.0 %collective-permute-start.2 = (f32[16,128]{1,0:T(8,128)S(1)}, f32[16,128]{1,0:T(8,128)S(1)}, u32[]{:S(2)}, u32[]{:S(2)}) collective-permute-start(f32[16,128]{1,0:T(8,128)S(1)} %add.12), channel_id=1, source_target_pairs={{0,64},{16,80},{32,96},{48,112},{64,0},{80,16},{96,32},{112,48},{1... | collective-permute-start | bytes 24584 | tf_op jit(solution)/shard_map/ppermute | solution.py:254
